TPU v7x, 128 devices: a whole 4x4x4 slice. The times are simulated.
128 devices in a mesh: band: 16 (over z, y), lon: 8 (over x, core).
Axes of the slice: x: 4, y: 4, z: 4, core: 2. Of those that a mesh axis runs over, the one named last changes fastest.
Arguments:
- background: float32 [2, 16, 1024, 256], P(None, None, ('lon', 'band')), may hold values from -6 to 6
- scale_x: float32 [16, 1024, 256], P(None, ('lon', 'band')), may hold values from 0.04 to 0.24
- scale_y: float32 [16, 1024, 256], P(None, ('lon', 'band')), may hold values from 0.04 to 0.24
- filter_bands: float32 [2, 5, 16], replicated, may hold values from -0.3 to 0.3
- band_rows: int32 [16], replicated, may hold values from 8 to 32, as said below
Outputs:
- increment: float32 [2, 16, 1024, 256], P(None, None, ('lon', 'band'))
- band_field: float32 [2, 16, 512, 1024], P(None, None, 'band', 'lon')
Inputs may be any that keep to these rules, and one draw needn't show every extreme that they name: `band_rows`: bands follow one another from the first row and their rows sum to 256; one band has exactly 32 rows and one exactly 8 rows.
All inputs are finite; a program needn't handle non-finite values.
Results may differ from a plain program's by a relative error of at most 0.0003.
Values sent between devices are 32-bit elements; how exact they have to be, the bound alone decides.
A program may use at most 64 MiB of HBM per device.

v0:
```python
import jax
import jax.numpy as jnp
from jax import lax
from jax.sharding import PartitionSpec as P

STEPS = 8
CAP = 32


def extended(block, sides, width, periodic):
    for axis, dim in sides:
        count = lax.axis_size(axis)
        forward = [(i, i + 1) for i in range(count - 1)]
        if periodic:
            forward.append((count - 1, 0))
        backward = [(target, source) for source, target in forward]
        low = lax.ppermute(
            lax.slice_in_dim(block, block.shape[dim] - width, None, axis=dim), axis, forward
        )
        high = lax.ppermute(lax.slice_in_dim(block, 0, width, axis=dim), axis, backward)
        block = jnp.concatenate([low, block, high], axis=dim)
    return block


def spread(field, along_x, along_y, x_axis, y_axis):
    flux_x = along_x * (jnp.roll(field, -1, x_axis) - field)
    flux_y = along_y * (jnp.roll(field, -1, y_axis) - field)
    return field + flux_x - jnp.roll(flux_x, 1, x_axis) + flux_y - jnp.roll(flux_y, 1, y_axis)


def vertical(field, filter_bands):
    levels = field.shape[1]
    padded = jnp.pad(field, ((0, 0), (2, 2), (0, 0), (0, 0)))
    total = field
    for offset in range(5):
        weight = filter_bands[:, offset, :][:, :, None, None]
        total = total + weight * padded[:, offset : offset + levels]
    return total


def cut_rows(block, starts, lengths):
    padded = jnp.pad(block, ((0, 0), (0, 0), (0, CAP)))

    def one_band(start, length):
        piece = lax.dynamic_slice_in_dim(padded, start, CAP, 2)
        keep = (jnp.arange(CAP) < length).astype(jnp.float32)
        return piece * keep

    return jax.vmap(one_band)(starts, lengths)


def unpack_bands(arrived):
    count, channels, width, height = arrived.shape
    return jnp.transpose(arrived, (1, 3, 0, 2)).reshape(channels, height, count * width)


def pack_strips(block, count):
    channels, height, columns = block.shape
    split = block.reshape(channels, height, count, columns // count)
    return jnp.transpose(split, (2, 0, 3, 1))


def place_rows(arrived, starts, total_rows):
    count, channels, width, height = arrived.shape
    empty = jnp.zeros((channels, width, total_rows + height), jnp.float32)

    def add_band(index, whole):
        current = lax.dynamic_slice_in_dim(whole, starts[index], height, 2)
        return lax.dynamic_update_slice_in_dim(whole, current + arrived[index], starts[index], 2)

    whole = lax.fori_loop(0, count, add_band, empty)
    return whole[:, :, :total_rows]


def band_margin(block, length_here, depth):
    wide = extended(block, (("lon", 2),), depth, True)
    channels, height, columns = wide.shape
    lower = lax.dynamic_slice_in_dim(wide, length_here - depth, depth, 1)
    edges = jnp.concatenate([wide[:, :depth], lower], 1)
    beside_all = extended(edges, (("band", 1),), depth, False)
    grown = jnp.concatenate(
        [beside_all[:, :depth], wide, jnp.zeros((channels, depth, columns), jnp.float32)], 1
    )
    return lax.dynamic_update_slice_in_dim(
        grown, beside_all[:, 3 * depth :], depth + length_here, 1
    )


def diffuse_bands(field, coefs, length_here, depth):
    channels, height, columns = field.shape
    grown_coefs = band_margin(coefs, length_here, depth)
    levels = coefs.shape[0] // 2
    keep = (jnp.arange(height) < length_here).astype(jnp.float32)[:, None]
    for round_index in range(STEPS // depth):
        grown = band_margin(field, length_here, depth)
        grown = grown.reshape((channels // levels, levels) + grown.shape[1:])
        for step in range(depth):
            grown = spread(grown, grown_coefs[:levels], grown_coefs[levels:], 3, 2)
        field = (
            grown[:, :, depth : depth + height, depth : depth + columns].reshape(field.shape) * keep
        )
    return field


def shards(background, scale_x, scale_y, filter_bands, band_rows):
    variables, levels, width, rows = background.shape
    count = lax.axis_size("band")
    along_y = scale_y * (jnp.arange(rows) < rows - 1).astype(jnp.float32)
    starts = jnp.cumsum(band_rows) - band_rows
    depth = 4
    stacked = background.reshape(variables * levels, width, rows)
    length_here = band_rows[lax.axis_index("band")]
    package = jnp.concatenate([stacked, scale_x, along_y], 0)
    sent = cut_rows(package, starts, band_rows)
    arrived = unpack_bands(lax.all_to_all(sent, "band", split_axis=0, concat_axis=0, tiled=True))
    field = diffuse_bands(
        arrived[: variables * levels], arrived[variables * levels :], length_here, depth
    )
    band_field = vertical(field.reshape(variables, levels, CAP, field.shape[2]), filter_bands)
    outgoing = pack_strips(band_field.reshape(variables * levels, CAP, field.shape[2]), count)
    returned = lax.all_to_all(outgoing, "band", split_axis=0, concat_axis=0, tiled=True)
    increment = place_rows(returned, starts, rows).reshape(background.shape)
    return (increment, band_field)


def solution(mesh):
    in_specs = (
        P(None, None, ("lon", "band"), None),
        P(None, ("lon", "band"), None),
        P(None, ("lon", "band"), None),
        P(),
        P(),
    )
    out_specs = (P(None, None, ("lon", "band"), None), P(None, None, "band", "lon"))
    return jax.shard_map(shards, mesh=mesh, in_specs=in_specs, out_specs=out_specs, check_vma=False)
```

profile of v0, /device:TPU:0, one launch (start us, length us, event | category | flops | bytes accessed | tf_op | source)
XLA Modules:
  0.0 343.5 jit_solution(2642964536780424236)
XLA Ops:
  12.0 3.4 reshape.105
  15.5 8.3 %all-to-all-start = ((f32[16,1,16384]{2,1,0:T(1,128)}), f32[16,1,16384]{2,1,0:T(1,128)S(1)}, u32[]{:S(2)}, u32[]{:S(2)}) async-start(f32[16,1,16384]{2,1,0:T(1,128)} %reshape.105), calls=%async_computation | async-start | bytes 2097152 | tf_op jit(solution)/shard_map/all_to_all | solution.py:115
  27.1 14.4 %all-to-all-done = f32[16,1,16384]{2,1,0:T(1,128)S(1)} async-done(((f32[16,1,16384]{2,1,0:T(1,128)}), f32[16,1,16384]{2,1,0:T(1,128)S(1)}, u32[]{:S(2)}, u32[]{:S(2)}) %all-to-all-start) | async-done | bytes 1048608 | tf_op jit(solution)/shard_map/all_to_all | solution.py:115
  42.0 3.1 reduce.1
  46.2 2.7 fusion.49
  48.9 3.1 copy.82
  52.1 2.9 collective-permute-start.1
  55.0 4.0 %copy.87 = f32[32,32,16,8]{1,3,2,0:T(8,128)} copy(f32[32,32,16,8]{0,3,1,2:T(8,128)} %get-tuple-element.128) | data formatting | bytes 1048576 | tf_op jit(solution)/shard_map/slice | solution.py:117
  60.0 2.9 collective-permute-start.5
  65.2 3.9 %fusion.46 = (f32[32,4,136]{1,2,0:T(8,128)}, f32[32,4,136]{1,2,0:T(8,128)}, f32[32,4,136]{1,2,0:T(8,128)}, f32[32,4,136]{1,2,0:T(8,128)S(1)}) fusion(f32[32,32,136]{1,2,0:T(8,128)S(1)} %pad_maximum_fusion.1, s32[]{:T(128)S(6)} %select_n.33, f32[32,32,136]{1,2,0:T(8,128)S(1)} %pad_maximum_fusion), kind=kLoop, calls=%fused_computation.106 | loop fusion | bytes 557060 | tf_op jit(solution)/shard_map/slice | solution.py:79
  69.1 2.8 copy.83
  73.9 2.8 copy.88
  76.8 2.1 collective-permute-start.6
  79.6 2.8 copy.90
  86.6 2.2 copy.84
  88.8 2.2 copy.89
  91.0 6.3 %maximum_maximum_fusion.1 = (f32[32,40,136]{1,2,0:T(8,128)}, f32[32,40,136]{1,2,0:T(8,128)S(1)}) fusion(f32[32,32,4]{1,2,0:T(4,128)S(1)} %collective-permute-done.5, f32[32,32,128]{1,2,0:T(8,128)} %bitcast.95, f32[32,32,4]{1,2,0:T(4,128)S(1)} %collective-permute-done.4, f32[32,4,136]{1,2,0:T(8,128)} %copy.89, f32[40]{0:T(128)S(1)} %pad.95.clone, ...), kind=kLoop, calls=%fused_computation.9 | loop fusion | flops 1392640 | bytes 2646176 | tf_op jit(solution)/shard_map/concatenate | solution.py:81
  97.2 2.2 copy.86
  99.4 14.1 %dynamic_update_slice.16 = f32[32,40,136]{1,2,0:T(8,128)S(1)} dynamic-update-slice(f32[32,40,136]{1,2,0:T(8,128)S(1)} %get-tuple-element.142, f32[32,4,136]{1,2,0:T(8,128)} %copy.86, s32[]{:T(128)} %constant.50.clone.1, s32[]{:T(128)S(6)} %select_n.34, s32[]{:T(128)} %constant.50.clone.1) | dynamic-update-slice | bytes 139268 | tf_op jit(solution)/shard_map/dynamic_update_slice | solution.py:84
  115.2 2.1 slice.404
  118.0 13.0 %dynamic_update_slice.17 = f32[32,40,136]{1,2,0:T(8,128)} dynamic-update-slice(f32[32,40,136]{1,2,0:T(8,128)} %get-tuple-element.141, f32[32,4,136]{1,2,0:T(8,128)S(1)} %copy.91, s32[]{:T(128)} %constant.50.clone.1, s32[]{:T(128)S(6)} %select_n.34, s32[]{:T(128)} %constant.50.clone.1) | dynamic-update-slice | bytes 139268 | tf_op jit(solution)/shard_map/dynamic_update_slice | solution.py:84
  134.0 2.6 fusion
  147.6 4.9 %fusion.40 = f32[2,16,32,128]{2,3,1,0:T(8,128)} fusion(f32[2,16,39,136]{2,3,1,0:T(8,128)S(1)} %bitcast.83, f32[2,16,1,136]{2,3,1,0:T(8,128)S(1)} %slice.430, f32[2,16,40,136]{2,3,1,0:T(8,128)S(1)} %get-tuple-element.113, f32[2,16,40,135]{2,3,1,0:T(8,128)S(1)} %bitcast.97, f32[2,16,40,1]{2,3,1,0:T(1,128)S(1)} %slice.426, ...), kind=kLoop, calls=%fused_computation.77 | loop fusion | flops 786432 | bytes 3489792 | tf_op jit(solution)/shard_map/sub | solution.py:28
  152.6 2.2 copy.92
  155.1 2.9 collective-permute-start.9
  158.1 6.9 %collective-permute-done.8 = f32[32,32,4]{2,1,0:T(8,128)S(1)} collective-permute-done((f32[32,32,4]{2,1,0:T(8,128)S(1)}, f32[32,32,4]{2,1,0:T(8,128)S(1)}, u32[]{:S(2)}, u32[]{:S(2)}) %collective-permute-start.8) | collective-permute-done | bytes 16416 | tf_op jit(solution)/shard_map/ppermute | solution.py:17
  165.5 5.2 %collective-permute-start.10 = (f32[32,4,136]{2,0,1:T(8,128)S(1)}, f32[32,4,136]{2,0,1:T(8,128)S(1)}, u32[]{:S(2)}, u32[]{:S(2)}) collective-permute-start(f32[32,4,136]{2,0,1:T(8,128)S(1)} %copy.101), channel_id=1, source_target_pairs={{0,8},{8,16},{16,24},{24,32},{32,40},{40,48},{48,56},{56,64},{64,7... | collective-permute-start | bytes 208904 | tf_op jit(solution)/shard_map/ppermute | solution.py:17
  173.9 4.3 %collective-permute-done.11 = f32[32,4,136]{2,0,1:T(8,128)S(1)} collective-permute-done((f32[32,4,136]{2,0,1:T(8,128)S(1)}, f32[32,4,136]{2,0,1:T(8,128)S(1)}, u32[]{:S(2)}, u32[]{:S(2)}) %collective-permute-start.11) | collective-permute-done | bytes 69664 | tf_op jit(solution)/shard_map/ppermute | solution.py:20
  197.1 3.6 %fusion.38 = f32[2,16,32,128]{2,3,1,0:T(8,128)S(1)} fusion(f32[2,16,39,136]{2,3,1,0:T(8,128)S(1)} %bitcast.84, f32[2,16,1,136]{2,3,1,0:T(8,128)S(1)} %slice.468, f32[2,16,40,136]{2,3,1,0:T(8,128)S(1)} %get-tuple-element.105, f32[2,16,40,135]{2,3,1,0:T(8,128)S(1)} %bitcast.98, f32[2,16,40,1]{2,3,1,0:T(1,128)S(1)} %slice.464, ...), kind=kLoop, calls=%fused_computation.71 | loop fusion | flops 917504 | bytes 3489920 | tf_op jit(solution)/shard_map/mul | solution.py:100
  203.6 3.1 reshape.107
  206.7 11.3 %all-to-all-start.1 = ((f32[16,1,8192]{2,1,0:T(1,128)}), f32[16,1,8192]{2,1,0:T(1,128)S(1)}, u32[]{:S(2)}, u32[]{:S(2)}) async-start(f32[16,1,8192]{2,1,0:T(1,128)} %reshape.107), calls=%async_computation.1 | async-start | bytes 1048576 | tf_op jit(solution)/shard_map/all_to_all | solution.py:121
  219.4 8.8 %all-to-all-done.1 = f32[16,1,8192]{2,1,0:T(1,128)S(1)} async-done(((f32[16,1,8192]{2,1,0:T(1,128)}), f32[16,1,8192]{2,1,0:T(1,128)S(1)}, u32[]{:S(2)}, u32[]{:S(2)}) %all-to-all-start.1) | async-done | bytes 524320 | tf_op jit(solution)/shard_map/all_to_all | solution.py:121
  230.7 111.8 %while.13 = (s32[]{:T(128)}, f32[32,8,288]{2,1,0:T(8,128)S(1)}, s32[16]{0:T(128)S(1)}, f32[16,32,8,32]{3,2,1,0:T(8,128)S(1)}, s32[]{:T(128)}, /*index=5*/s32[]{:T(128)}, s32[]{:T(128)}) while((s32[]{:T(128)}, f32[32,8,288]{2,1,0:T(8,128)S(1)}, s32[16]{0:T(128)S(1)}, f32[16,32,8,32]{3,2,1,0:T(8,128)S(1)}, s32[]{:T(128)}, /*index=5*/s32[]{:T(128)}, ...), condition=%wide.region_2.3_spmd, body=%wide.region_1.2_spmd.sunk | while | flops 8197 | bytes 163975 | solution.py:71
  236.1 4.8 %dynamic_update_slice.20 = f32[32,8,288]{2,1,0:T(8,128)S(1)} dynamic-update-slice(f32[32,8,288]{2,1,0:T(8,128)S(1)} %get-tuple-element.178, f32[32,8,32]{2,1,0:T(8,128)S(1)} %bitcast_add_fusion.2, s32[]{:T(128)} %constant.50.clone.1..sunk, s32[]{:T(128)} %constant.50.clone.1..sunk, s32[]{:T(128)S(6)} %select_n.41) | dynamic-update-slice | bytes 65540 | tf_op jit(solution)/shard_map/while/body/eval_jaxpr/dynamic_update_slice | solution.py:69
  243.3 4.8 %dynamic_update_slice.20 = f32[32,8,288]{2,1,0:T(8,128)S(1)} dynamic-update-slice(f32[32,8,288]{2,1,0:T(8,128)S(1)} %get-tuple-element.178, f32[32,8,32]{2,1,0:T(8,128)S(1)} %bitcast_add_fusion.2, s32[]{:T(128)} %constant.50.clone.1..sunk, s32[]{:T(128)} %constant.50.clone.1..sunk, s32[]{:T(128)S(6)} %select_n.41) | dynamic-update-slice | bytes 65540 | tf_op jit(solution)/shard_map/while/body/eval_jaxpr/dynamic_update_slice | solution.py:69
  250.6 4.8 %dynamic_update_slice.20 = f32[32,8,288]{2,1,0:T(8,128)S(1)} dynamic-update-slice(f32[32,8,288]{2,1,0:T(8,128)S(1)} %get-tuple-element.178, f32[32,8,32]{2,1,0:T(8,128)S(1)} %bitcast_add_fusion.2, s32[]{:T(128)} %constant.50.clone.1..sunk, s32[]{:T(128)} %constant.50.clone.1..sunk, s32[]{:T(128)S(6)} %select_n.41) | dynamic-update-slice | bytes 65540 | tf_op jit(solution)/shard_map/while/body/eval_jaxpr/dynamic_update_slice | solution.py:69
  257.8 4.8 %dynamic_update_slice.20 = f32[32,8,288]{2,1,0:T(8,128)S(1)} dynamic-update-slice(f32[32,8,288]{2,1,0:T(8,128)S(1)} %get-tuple-element.178, f32[32,8,32]{2,1,0:T(8,128)S(1)} %bitcast_add_fusion.2, s32[]{:T(128)} %constant.50.clone.1..sunk, s32[]{:T(128)} %constant.50.clone.1..sunk, s32[]{:T(128)S(6)} %select_n.41) | dynamic-update-slice | bytes 65540 | tf_op jit(solution)/shard_map/while/body/eval_jaxpr/dynamic_update_slice | solution.py:69
  265.1 4.8 %dynamic_update_slice.20 = f32[32,8,288]{2,1,0:T(8,128)S(1)} dynamic-update-slice(f32[32,8,288]{2,1,0:T(8,128)S(1)} %get-tuple-element.178, f32[32,8,32]{2,1,0:T(8,128)S(1)} %bitcast_add_fusion.2, s32[]{:T(128)} %constant.50.clone.1..sunk, s32[]{:T(128)} %constant.50.clone.1..sunk, s32[]{:T(128)S(6)} %select_n.41) | dynamic-update-slice | bytes 65540 | tf_op jit(solution)/shard_map/while/body/eval_jaxpr/dynamic_update_slice | solution.py:69
  272.4 4.8 %dynamic_update_slice.20 = f32[32,8,288]{2,1,0:T(8,128)S(1)} dynamic-update-slice(f32[32,8,288]{2,1,0:T(8,128)S(1)} %get-tuple-element.178, f32[32,8,32]{2,1,0:T(8,128)S(1)} %bitcast_add_fusion.2, s32[]{:T(128)} %constant.50.clone.1..sunk, s32[]{:T(128)} %constant.50.clone.1..sunk, s32[]{:T(128)S(6)} %select_n.41) | dynamic-update-slice | bytes 65540 | tf_op jit(solution)/shard_map/while/body/eval_jaxpr/dynamic_update_slice | solution.py:69
  279.6 4.8 %dynamic_update_slice.20 = f32[32,8,288]{2,1,0:T(8,128)S(1)} dynamic-update-slice(f32[32,8,288]{2,1,0:T(8,128)S(1)} %get-tuple-element.178, f32[32,8,32]{2,1,0:T(8,128)S(1)} %bitcast_add_fusion.2, s32[]{:T(128)} %constant.50.clone.1..sunk, s32[]{:T(128)} %constant.50.clone.1..sunk, s32[]{:T(128)S(6)} %select_n.41) | dynamic-update-slice | bytes 65540 | tf_op jit(solution)/shard_map/while/body/eval_jaxpr/dynamic_update_slice | solution.py:69
  286.9 4.8 %dynamic_update_slice.20 = f32[32,8,288]{2,1,0:T(8,128)S(1)} dynamic-update-slice(f32[32,8,288]{2,1,0:T(8,128)S(1)} %get-tuple-element.178, f32[32,8,32]{2,1,0:T(8,128)S(1)} %bitcast_add_fusion.2, s32[]{:T(128)} %constant.50.clone.1..sunk, s32[]{:T(128)} %constant.50.clone.1..sunk, s32[]{:T(128)S(6)} %select_n.41) | dynamic-update-slice | bytes 65540 | tf_op jit(solution)/shard_map/while/body/eval_jaxpr/dynamic_update_slice | solution.py:69
  294.1 4.8 %dynamic_update_slice.20 = f32[32,8,288]{2,1,0:T(8,128)S(1)} dynamic-update-slice(f32[32,8,288]{2,1,0:T(8,128)S(1)} %get-tuple-element.178, f32[32,8,32]{2,1,0:T(8,128)S(1)} %bitcast_add_fusion.2, s32[]{:T(128)} %constant.50.clone.1..sunk, s32[]{:T(128)} %constant.50.clone.1..sunk, s32[]{:T(128)S(6)} %select_n.41) | dynamic-update-slice | bytes 65540 | tf_op jit(solution)/shard_map/while/body/eval_jaxpr/dynamic_update_slice | solution.py:69
  301.4 4.8 %dynamic_update_slice.20 = f32[32,8,288]{2,1,0:T(8,128)S(1)} dynamic-update-slice(f32[32,8,288]{2,1,0:T(8,128)S(1)} %get-tuple-element.178, f32[32,8,32]{2,1,0:T(8,128)S(1)} %bitcast_add_fusion.2, s32[]{:T(128)} %constant.50.clone.1..sunk, s32[]{:T(128)} %constant.50.clone.1..sunk, s32[]{:T(128)S(6)} %select_n.41) | dynamic-update-slice | bytes 65540 | tf_op jit(solution)/shard_map/while/body/eval_jaxpr/dynamic_update_slice | solution.py:69
  308.6 4.8 %dynamic_update_slice.20 = f32[32,8,288]{2,1,0:T(8,128)S(1)} dynamic-update-slice(f32[32,8,288]{2,1,0:T(8,128)S(1)} %get-tuple-element.178, f32[32,8,32]{2,1,0:T(8,128)S(1)} %bitcast_add_fusion.2, s32[]{:T(128)} %constant.50.clone.1..sunk, s32[]{:T(128)} %constant.50.clone.1..sunk, s32[]{:T(128)S(6)} %select_n.41) | dynamic-update-slice | bytes 65540 | tf_op jit(solution)/shard_map/while/body/eval_jaxpr/dynamic_update_slice | solution.py:69
  315.9 4.8 %dynamic_update_slice.20 = f32[32,8,288]{2,1,0:T(8,128)S(1)} dynamic-update-slice(f32[32,8,288]{2,1,0:T(8,128)S(1)} %get-tuple-element.178, f32[32,8,32]{2,1,0:T(8,128)S(1)} %bitcast_add_fusion.2, s32[]{:T(128)} %constant.50.clone.1..sunk, s32[]{:T(128)} %constant.50.clone.1..sunk, s32[]{:T(128)S(6)} %select_n.41) | dynamic-update-slice | bytes 65540 | tf_op jit(solution)/shard_map/while/body/eval_jaxpr/dynamic_update_slice | solution.py:69
  323.2 4.8 %dynamic_update_slice.20 = f32[32,8,288]{2,1,0:T(8,128)S(1)} dynamic-update-slice(f32[32,8,288]{2,1,0:T(8,128)S(1)} %get-tuple-element.178, f32[32,8,32]{2,1,0:T(8,128)S(1)} %bitcast_add_fusion.2, s32[]{:T(128)} %constant.50.clone.1..sunk, s32[]{:T(128)} %constant.50.clone.1..sunk, s32[]{:T(128)S(6)} %select_n.41) | dynamic-update-slice | bytes 65540 | tf_op jit(solution)/shard_map/while/body/eval_jaxpr/dynamic_update_slice | solution.py:69
  330.4 4.8 %dynamic_update_slice.20 = f32[32,8,288]{2,1,0:T(8,128)S(1)} dynamic-update-slice(f32[32,8,288]{2,1,0:T(8,128)S(1)} %get-tuple-element.178, f32[32,8,32]{2,1,0:T(8,128)S(1)} %bitcast_add_fusion.2, s32[]{:T(128)} %constant.50.clone.1..sunk, s32[]{:T(128)} %constant.50.clone.1..sunk, s32[]{:T(128)S(6)} %select_n.41) | dynamic-update-slice | bytes 65540 | tf_op jit(solution)/shard_map/while/body/eval_jaxpr/dynamic_update_slice | solution.py:69
  337.7 4.8 %dynamic_update_slice.20 = f32[32,8,288]{2,1,0:T(8,128)S(1)} dynamic-update-slice(f32[32,8,288]{2,1,0:T(8,128)S(1)} %get-tuple-element.178, f32[32,8,32]{2,1,0:T(8,128)S(1)} %bitcast_add_fusion.2, s32[]{:T(128)} %constant.50.clone.1..sunk, s32[]{:T(128)} %constant.50.clone.1..sunk, s32[]{:T(128)S(6)} %select_n.41) | dynamic-update-slice | bytes 65540 | tf_op jit(solution)/shard_map/while/body/eval_jaxpr/dynamic_update_slice | solution.py:69
  (178 shorter events, 81.9 us)
Async XLA Ops:
  0.6 5.6 %copy-start.6 = (f32[16,8,256]{2,1,0:T(8,128)S(1)}, f32[16,8,256]{2,1,0:T(8,128)}, u32[]{:S(2)}) copy-start(f32[16,8,256]{2,1,0:T(8,128)} %param.8) | copy-start | bytes 393220
  12.0 11.8 %copy-start.8 = (s32[16]{0:T(128)S(1)}, s32[16]{0:T(128)}, u32[]{:S(2)}) copy-start(s32[16]{0:T(128)} %param.11) | copy-start | bytes 196
  15.5 26.0 %all-to-all-start = ((f32[16,1,16384]{2,1,0:T(1,128)}), f32[16,1,16384]{2,1,0:T(1,128)S(1)}, u32[]{:S(2)}, u32[]{:S(2)}) async-start(f32[16,1,16384]{2,1,0:T(1,128)} %reshape.105), calls=%async_computation | async-start | bytes 2097152 | tf_op jit(solution)/shard_map/all_to_all | solution.py:115
  27.1 63.9 %copy-start.12 = (f32[40]{0:T(128)}, f32[40]{0:T(128)S(1)}, u32[]{:S(2)}) copy-start(f32[40]{0:T(128)S(1)} %pad.95.clone) | copy-start | bytes 484
  52.0 10.9 %copy-start.3 = (f32[32,32,16,8]{1,3,2,0:T(8,128)}, f32[32,32,16,8]{1,3,2,0:T(8,128)S(1)}, u32[]{:S(2)}) copy-start(f32[32,32,16,8]{1,3,2,0:T(8,128)S(1)} %copy.82) | copy-start | bytes 1572868
  52.1 10.9 %collective-permute-start = (f32[32,32,4]{1,2,0:T(4,128)S(1)}, f32[32,32,4]{1,2,0:T(4,128)S(1)}, u32[]{:S(2)}, u32[]{:S(2)}) collective-permute-start(f32[32,32,4]{1,2,0:T(4,128)S(1)} %get-tuple-element.130), channel_id=1, source_target_pairs={{0,1},{1,2},{2,3},{3,4},{4,5},{5,6},{6,7},{7,0},{8,9},{9,10},{10,1... | collective-permute-start | bytes 49160 | tf_op jit(solution)/shard_map/ppermute | solution.py:17
  52.1 10.9 %collective-permute-start.1 = (f32[32,32,4]{1,2,0:T(4,128)S(1)}, f32[32,32,4]{1,2,0:T(4,128)S(1)}, u32[]{:S(2)}, u32[]{:S(2)}) collective-permute-start(f32[32,32,4]{1,2,0:T(4,128)S(1)} %get-tuple-element.131), channel_id=1, source_target_pairs={{1,0},{2,1},{3,2},{4,3},{5,4},{6,5},{7,6},{0,7},{9,8},{10,9},{11,1... | collective-permute-start | bytes 49160 | tf_op jit(solution)/shard_map/ppermute | solution.py:20
  60.0 4.9 %collective-permute-start.4 = (f32[32,32,4]{1,2,0:T(4,128)S(1)}, f32[32,32,4]{1,2,0:T(4,128)S(1)}, u32[]{:S(2)}, u32[]{:S(2)}) collective-permute-start(f32[32,32,4]{1,2,0:T(4,128)S(1)} %get-tuple-element.126), channel_id=1, source_target_pairs={{0,1},{1,2},{2,3},{3,4},{4,5},{5,6},{6,7},{7,0},{8,9},{9,10},{10,1... | collective-permute-start | bytes 49160 | tf_op jit(solution)/shard_map/ppermute | solution.py:17
  60.0 4.9 %copy-start.4 = (f32[32,32,16,8]{1,3,2,0:T(8,128)S(1)}, f32[32,32,16,8]{1,3,2,0:T(8,128)}, u32[]{:S(2)}) copy-start(f32[32,32,16,8]{1,3,2,0:T(8,128)} %copy.87) | copy-start | bytes 1572868
  60.0 4.9 %collective-permute-start.5 = (f32[32,32,4]{1,2,0:T(4,128)S(1)}, f32[32,32,4]{1,2,0:T(4,128)S(1)}, u32[]{:S(2)}, u32[]{:S(2)}) collective-permute-start(f32[32,32,4]{1,2,0:T(4,128)S(1)} %get-tuple-element.127), channel_id=1, source_target_pairs={{1,0},{2,1},{3,2},{4,3},{5,4},{6,5},{7,6},{0,7},{9,8},{10,9},{11,1... | collective-permute-start | bytes 49160 | tf_op jit(solution)/shard_map/ppermute | solution.py:20
  72.0 14.7 %collective-permute-start.2 = (f32[32,4,136]{2,0,1:T(8,128)S(1)}, f32[32,4,136]{2,0,1:T(8,128)S(1)}, u32[]{:S(2)}, u32[]{:S(2)}) collective-permute-start(f32[32,4,136]{2,0,1:T(8,128)S(1)} %copy.83), channel_id=1, source_target_pairs={{0,8},{8,16},{16,24},{24,32},{32,40},{40,48},{48,56},{56,64},{64,7... | collective-permute-start | bytes 208904 | tf_op jit(solution)/shard_map/ppermute | solution.py:17
  76.8 12.0 %collective-permute-start.6 = (f32[32,4,136]{2,0,1:T(8,128)S(1)}, f32[32,4,136]{2,0,1:T(8,128)S(1)}, u32[]{:S(2)}, u32[]{:S(2)}) collective-permute-start(f32[32,4,136]{2,0,1:T(8,128)S(1)} %copy.88), channel_id=1, source_target_pairs={{0,8},{8,16},{16,24},{24,32},{32,40},{40,48},{48,56},{56,64},{64,7... | collective-permute-start | bytes 208904 | tf_op jit(solution)/shard_map/ppermute | solution.py:17
  79.5 75.2 %copy-start.10 = (f32[32]{0:T(128)}, f32[32]{0:T(128)S(1)}, u32[]{:S(2)}) copy-start(f32[32]{0:T(128)S(1)} %compare_convert_fusion) | copy-start | bytes 388
  82.4 34.9 %collective-permute-start.7 = (f32[32,4,136]{2,0,1:T(8,128)S(1)}, f32[32,4,136]{2,0,1:T(8,128)S(1)}, u32[]{:S(2)}, u32[]{:S(2)}) collective-permute-start(f32[32,4,136]{2,0,1:T(8,128)S(1)} %copy.90), channel_id=1, source_target_pairs={{8,0},{16,8},{24,16},{32,24},{40,32},{48,40},{56,48},{64,56},{72,6... | collective-permute-start | bytes 208904 | tf_op jit(solution)/shard_map/ppermute | solution.py:20
  84.9 12.3 %collective-permute-start.3 = (f32[32,4,136]{2,0,1:T(8,128)S(1)}, f32[32,4,136]{2,0,1:T(8,128)S(1)}, u32[]{:S(2)}, u32[]{:S(2)}) collective-permute-start(f32[32,4,136]{2,0,1:T(8,128)S(1)} %copy.85), channel_id=1, source_target_pairs={{8,0},{16,8},{24,16},{32,24},{40,32},{48,40},{56,48},{64,56},{72,6... | collective-permute-start | bytes 208904 | tf_op jit(solution)/shard_map/ppermute | solution.py:20
  113.5 3.7 %copy-start = (f32[32,40,136]{1,2,0:T(8,128)}, f32[32,40,136]{1,2,0:T(8,128)S(1)}, u32[]{:S(2)}) copy-start(f32[32,40,136]{1,2,0:T(8,128)S(1)} %dynamic_update_slice.16) | copy-start | bytes 2088964
  131.0 2.3 copy-start.1
  131.0 3.0 copy-start.5
  155.1 15.6 %copy-start.7 = (f32[2,5,16]{2,0,1:T(2,128)S(1)}, f32[2,5,16]{2,0,1:T(2,128)}, u32[]{:S(2)}) copy-start(f32[2,5,16]{2,0,1:T(2,128)} %param.10) | copy-start | bytes 1924
  155.1 18.2 %copy-start.13 = (f32[40]{0:T(128)S(1)}, f32[40]{0:T(128)}, u32[]{:S(2)}) copy-start(f32[40]{0:T(128)} %copy-done.12) | copy-start | bytes 484
  155.1 9.8 %collective-permute-start.8 = (f32[32,32,4]{2,1,0:T(8,128)S(1)}, f32[32,32,4]{2,1,0:T(8,128)S(1)}, u32[]{:S(2)}, u32[]{:S(2)}) collective-permute-start(f32[32,32,4]{2,1,0:T(8,128)S(1)} %get-tuple-element.134), channel_id=1, source_target_pairs={{0,1},{1,2},{2,3},{3,4},{4,5},{5,6},{6,7},{7,0},{8,9},{9,10},{10,1... | collective-permute-start | bytes 49160 | tf_op jit(solution)/shard_map/ppermute | solution.py:17
  155.1 9.8 %collective-permute-start.9 = (f32[32,32,4]{2,1,0:T(8,128)S(1)}, f32[32,32,4]{2,1,0:T(8,128)S(1)}, u32[]{:S(2)}, u32[]{:S(2)}) collective-permute-start(f32[32,32,4]{2,1,0:T(8,128)S(1)} %get-tuple-element.135), channel_id=1, source_target_pairs={{1,0},{2,1},{3,2},{4,3},{5,4},{6,5},{7,6},{0,7},{9,8},{10,9},{11,1... | collective-permute-start | bytes 49160 | tf_op jit(solution)/shard_map/ppermute | solution.py:20
  165.5 7.7 %collective-permute-start.10 = (f32[32,4,136]{2,0,1:T(8,128)S(1)}, f32[32,4,136]{2,0,1:T(8,128)S(1)}, u32[]{:S(2)}, u32[]{:S(2)}) collective-permute-start(f32[32,4,136]{2,0,1:T(8,128)S(1)} %copy.101), channel_id=1, source_target_pairs={{0,8},{8,16},{16,24},{24,32},{32,40},{40,48},{48,56},{56,64},{64,7... | collective-permute-start | bytes 208904 | tf_op jit(solution)/shard_map/ppermute | solution.py:17
  171.3 6.9 %collective-permute-start.11 = (f32[32,4,136]{2,0,1:T(8,128)S(1)}, f32[32,4,136]{2,0,1:T(8,128)S(1)}, u32[]{:S(2)}, u32[]{:S(2)}) collective-permute-start(f32[32,4,136]{2,0,1:T(8,128)S(1)} %copy.102), channel_id=1, source_target_pairs={{8,0},{16,8},{24,16},{32,24},{40,32},{48,40},{56,48},{64,56},{72,6... | collective-permute-start | bytes 208904 | tf_op jit(solution)/shard_map/ppermute | solution.py:20
  182.1 2.3 copy-start.2
  196.4 0.7 copy-start.11
  197.1 3.6 %copy-start.9 = (f32[2,16]{1,0:T(2,128)S(1)}, f32[2,16]{1,0:T(2,128)}, u32[]{:S(2)}) copy-start(f32[2,16]{1,0:T(2,128)} %get-tuple-element.140) | copy-start | bytes 388
  206.7 21.4 %all-to-all-start.1 = ((f32[16,1,8192]{2,1,0:T(1,128)}), f32[16,1,8192]{2,1,0:T(1,128)S(1)}, u32[]{:S(2)}, u32[]{:S(2)}) async-start(f32[16,1,8192]{2,1,0:T(1,128)} %reshape.107), calls=%async_computation.1 | async-start | bytes 1048576 | tf_op jit(solution)/shard_map/all_to_all | solution.py:121
  219.4 11.3 %copy-start.14 = (s32[16]{0:T(128)S(1)}, s32[16]{0:T(128)}, u32[]{:S(2)}) copy-start(s32[16]{0:T(128)} %get-tuple-element.172) | copy-start | bytes 196
where the time goes:
time: 348 us; the launch traced here: 343 us
  local copies, waits for them, and re-layouts  186 us (53%)
  other arithmetic  47.4 us (14%)
  starting transfers between devices  42 us (12%)
  waiting for transfers between devices  36.5 us (10%)
  loops' own time  27.8 us (8%)
  between operations  4.14 us (1%)
    dynamic_update_slice x16, local copies, waits for them, and re-layouts, add_band(): lax.dynamic_update_slice_in_dim(whole, current + arrived[index], starts[i...  73 us
    dynamic_update_slice x4, local copies, waits for them, and re-layouts, band_margin(): lax.dynamic_update_slice_in_dim(grown, beside_all[:, 3 * depth:], depth +...  30.2 us
    another operation x1, loops' own time, place_rows(): whole = lax.fori_loop(0, count, add_band, empty)  27.8 us
    all_to_all x1, waiting for transfers between devices, shards(): lax.all_to_all(sent, 'band', split_axis=0, concat_axis=0, tiled=True)  14.4 us
    ppermute x6, starting transfers between devices, extended(): lax.ppermute(lax.slice_in_dim(block, 0, width, axis=dim), axis, backward)  13.1 us
    unnamed x38, local copies, waits for them, and re-layouts  12.3 us
    all_to_all x1, starting transfers between devices, shards(): lax.all_to_all(outgoing, 'band', split_axis=0, concat_axis=0, tiled=True)  11.3 us
    sub x7, other arithmetic, spread(): field + flux_x - jnp.roll(flux_x, 1, x_axis) + flux_y  11 us
  transfers between devices with their start and end apart: 14, of which 6 were waited for; matrix products, arithmetic and copies ran while one was open for 14% of the time, Pallas kernels for 0%

commit v1 on v0

v1 whole, which is shorter than its diff:
```python
import functools

import jax
import jax.numpy as jnp
from jax import lax
from jax.experimental import pallas as pl
from jax.experimental.pallas import tpu as pltpu
from jax.sharding import PartitionSpec as P

MESH = pl.DeviceIdType.MESH
STEPS = 8
CAP = 32
DEPTH = 4
ROUNDS = STEPS // DEPTH
WIDTH = 8
LANES = 128
SX, SY = 2, 3


def roll(x, shift):
    return pltpu.roll(x, shift, x.ndim - 1)


def diffuse(get_field, get_sx, get_sy, put, lane):
    last, first = lane == LANES - 1, lane == 0
    held = [None] * DEPTH
    flux = [None] * DEPTH

    def push(step, column, field):
        if step == DEPTH:
            put(column, field)
            return
        before, west = held[step], flux[step]
        held[step] = field
        if before is None:
            return
        p = column - 1
        sx = get_sx(p)
        east = [sx[i] * (field[i] - before[i]) for i in range(2)]
        flux[step] = east
        if west is None:
            return
        sy = get_sy(p)
        ra, rb = roll(before[0], LANES - 1), roll(before[1], LANES - 1)
        up = [jnp.where(last, rb, ra), rb]
        north = [sy[i] * (up[i] - before[i]) for i in range(2)]
        qa, qb = roll(north[0], 1), roll(north[1], 1)
        south = [jnp.where(first, qb, qa), jnp.where(first, qa, qb)]
        new = [before[i] + east[i] - west[i] + north[i] - south[i] for i in range(2)]
        push(step + 1, p, new)

    for column in range(-DEPTH, WIDTH + DEPTH):
        push(0, column, get_field(column))


def kernel(
    rows_ref, filt_ref, bg_ref, sx_ref, sy_ref,
    inc_ref, bf_ref,
    raw_bg, raw_sx, raw_sy, own, halo0, halo1, mid, done, nat, out_inc,
    send_buf, recv_buf, band_nat, out_bf, st,
    in_sem, hs_sem, hr_sem, as_sem, ar_sem, out_sem,
):
    n_band, n_lon = lax.axis_size("band"), lax.axis_size("lon")
    band, lon = lax.axis_index("band"), lax.axis_index("lon")
    at_end, at_start = band == n_band - 1, band == 0
    right = (
        jnp.where(at_end, 0, band + 1),
        jnp.where(at_end, lax.rem(lon + 1, n_lon), lon),
    )
    left = (
        jnp.where(at_start, n_band - 1, band - 1),
        jnp.where(at_start, lax.rem(lon + n_lon - 1, n_lon), lon),
    )

    def peer(k):
        z = lax.rem(band // 4 + k // 4, 4)
        y = lax.rem(lax.rem(band, 4) + lax.rem(k, 4), 4)
        return z * 4 + y

    barrier = pltpu.get_barrier_semaphore()
    for side in (left, right):
        pl.semaphore_signal(barrier, inc=1, device_id=side, device_id_type=MESH)

    def greet(k, carry):
        pl.semaphore_signal(
            barrier, inc=1, device_id=(peer(k), lon), device_id_type=MESH
        )
        return carry

    lax.fori_loop(1, n_band, greet, 0)

    copies = []
    for ref, raw in ((bg_ref, raw_bg), (sx_ref, raw_sx), (sy_ref, raw_sy)):
        for half in range(2):
            copies.append(
                pltpu.make_async_copy(
                    ref.at[:, pl.ds(half * LANES, LANES)],
                    raw.at[half],
                    in_sem.at[len(copies)],
                )
            )
            copies[-1].start()

    total = jnp.int32(0)
    for b in range(16):
        st[b] = total
        total = total + rows_ref[b]

    lane = lax.broadcasted_iota(jnp.int32, (8, LANES), 1)
    lane2 = lax.broadcasted_iota(jnp.int32, (2, 8, LANES), 2)
    for copy in copies:
        copy.wait()
    for h in range(2):
        for c in range(WIDTH):
            for half in range(2):
                for v in range(2):
                    own[h, c, v, half] = raw_bg[half, pl.ds(v * 128 + h * 64 + c, 8, stride=8), :]
                own[h, c, SX, half] = raw_sx[half, pl.ds(h * 64 + c, 8, stride=8), :]
                face = raw_sy[half, pl.ds(h * 64 + c, 8, stride=8), :]
                if half == 1:
                    face = jnp.where(lane == LANES - 1, 0.0, face)
                own[h, c, SY, half] = face

    pl.semaphore_wait(barrier, 2 + 15)

    def halo_copies(r, h):
        src, dst = ((own, halo0), (mid, halo1))[r]
        return [
            pltpu.make_async_remote_copy(
                src_ref=src.at[h, pl.ds(0, DEPTH)],
                dst_ref=dst.at[h, 1],
                send_sem=hs_sem.at[r, h, 0],
                recv_sem=hr_sem.at[r, h, 1],
                device_id=left,
                device_id_type=MESH,
            ),
            pltpu.make_async_remote_copy(
                src_ref=src.at[h, pl.ds(WIDTH - DEPTH, DEPTH)],
                dst_ref=dst.at[h, 0],
                send_sem=hs_sem.at[r, h, 1],
                recv_sem=hr_sem.at[r, h, 0],
                device_id=right,
                device_id_type=MESH,
            ),
        ]

    for h in range(2):
        for copy in halo_copies(0, h):
            copy.start()

    def one_round(r, h):
        inner, halo = ((own, halo0), (mid, halo1))[r]

        def pick(mine, side, column, unit):
            if column < 0:
                at = (h, 0, column + DEPTH)
                ref = side
            elif column < WIDTH:
                at = (h, column)
                ref = mine
            else:
                at = (h, 1, column - WIDTH)
                ref = side
            return [ref[at + (unit, half)] for half in range(2)]

        def put(column, new):
            if r + 1 < ROUNDS:
                for half in range(2):
                    mid[h, column, :, half] = new[half]
                return
            for half in range(2):
                done[h, column, :, half] = new[half]
                for v in range(2):
                    nat[half, pl.ds(v * 128 + h * 64 + column, 8, stride=8), :] = new[half][v]

        diffuse(
            lambda column: pick(inner, halo, column, slice(0, 2)),
            lambda column: pick(own, halo0, column, SX),
            lambda column: pick(own, halo0, column, SY),
            put,
            lane,
        )

    for h in range(2):
        for copy in halo_copies(0, h):
            copy.wait_recv()
        one_round(0, h)
        for copy in halo_copies(1, h):
            copy.start()
    for h in range(2):
        for copy in halo_copies(1, h):
            copy.wait_recv()
        one_round(1, h)

    def window(b, keep):
        start = st[b]
        for c in range(WIDTH):
            parts = []
            for q in range(4):
                v, h = q // 2, q % 2
                x = jnp.where(lane >= start, done[h, c, v, 0], done[h, c, v, 1])
                parts.append(roll(x, (32 * q + 256 - start) & 127))
            keep(
                c,
                jnp.where(
                    lane < 64,
                    jnp.where(lane < 32, parts[0], parts[1]),
                    jnp.where(lane < 96, parts[2], parts[3]),
                ),
            )

    def band_copy(k):
        return pltpu.make_async_remote_copy(
            src_ref=send_buf.at[k],
            dst_ref=recv_buf.at[pl.ds(pl.multiple_of(band * 64, 64), 64)],
            send_sem=as_sem.at[k],
            recv_sem=ar_sem.at[k],
            device_id=(peer(k), lon),
            device_id_type=MESH,
        )

    def send(k, carry):
        def keep(c, value):
            send_buf[k, pl.ds(c * 8, 8), :] = value

        window(peer(k), keep)
        band_copy(k).start()
        return carry

    lax.fori_loop(1, n_band, send, 0)

    def keep_own(c, value):
        recv_buf[pl.ds(pl.multiple_of(band * 64 + c * 8, 8), 8), :] = value

    window(band, keep_own)

    for v in range(2):
        for level in range(16):
            for half in range(2):
                rows = v * 128 + level * 8
                value = nat[half, rows:rows + 8, :]
                for o in range(5):
                    if 0 <= level + o - 2 < 16:
                        near = rows + (o - 2) * 8
                        value = value + filt_ref[o, v, level] * nat[half, near:near + 8, :]
                out_inc[rows:rows + 8, half * LANES:(half + 1) * LANES] = value
    put_inc = pltpu.make_async_copy(out_inc, inc_ref, out_sem.at[0])
    put_inc.start()

    def arrive(k, carry):
        band_copy(k).wait_recv()
        return carry

    lax.fori_loop(1, n_band, arrive, 0)

    for s in range(8):
        flat = recv_buf[pl.ds(s, LANES, stride=8), :].T
        for q in range(4):
            v, h = q // 2, q % 2
            band_nat[v, h * 8 + s] = flat[q * CAP:(q + 1) * CAP, :]
    inside = lax.broadcasted_iota(jnp.int32, (CAP, LANES), 0) < rows_ref[band]
    outs = []
    for v in range(2):
        for level in range(16):
            value = band_nat[v, level]
            for o in range(5):
                if 0 <= level + o - 2 < 16:
                    value = value + filt_ref[o, v, level] * band_nat[v, level + o - 2]
            rows = (v * 16 + level) * CAP
            out_bf[rows:rows + CAP, :] = jnp.where(inside, value, 0.0)
        copy = pltpu.make_async_copy(
            out_bf.at[pl.ds(v * 512, 512)], bf_ref.at[pl.ds(v * 512, 512)], out_sem.at[1 + v]
        )
        copy.start()
        outs.append(copy)

    for r in range(ROUNDS):
        for h in range(2):
            for copy in halo_copies(r, h):
                copy.wait_send()

    def sent(k, carry):
        band_copy(k).wait_send()
        return carry

    lax.fori_loop(1, n_band, sent, 0)
    put_inc.wait()
    for copy in outs:
        copy.wait()


def shards(background, scale_x, scale_y, filter_bands, band_rows):
    f32 = jnp.float32
    any_space = pl.BlockSpec(memory_space=pl.ANY)
    smem = pl.BlockSpec(memory_space=pltpu.SMEM)
    vmem = pltpu.VMEM
    dma = pltpu.SemaphoreType.DMA
    inc, bf = pl.pallas_call(
        kernel,
        out_shape=(
            jax.ShapeDtypeStruct((256, 256), f32),
            jax.ShapeDtypeStruct((1024, LANES), f32),
        ),
        in_specs=[smem, smem, any_space, any_space, any_space],
        out_specs=(any_space, any_space),
        scratch_shapes=[
            vmem((2, 256, LANES), f32),
            vmem((2, 128, LANES), f32),
            vmem((2, 128, LANES), f32),
            vmem((2, WIDTH, 4, 2, 8, LANES), f32),
            vmem((2, 2, DEPTH, 4, 2, 8, LANES), f32),
            vmem((2, 2, DEPTH, 2, 2, 8, LANES), f32),
            vmem((2, WIDTH, 2, 2, 8, LANES), f32),
            vmem((2, WIDTH, 2, 2, 8, LANES), f32),
            vmem((2, 256, LANES), f32),
            vmem((256, 256), f32),
            vmem((16, 64, LANES), f32),
            vmem((1024, LANES), f32),
            vmem((2, 16, CAP, LANES), f32),
            vmem((1024, LANES), f32),
            pltpu.SMEM((16,), jnp.int32),
            dma((6,)),
            dma((ROUNDS, 2, 2)),
            dma((ROUNDS, 2, 2)),
            dma((16,)),
            dma((16,)),
            dma((3,)),
        ],
        compiler_params=pltpu.CompilerParams(collective_id=0, has_side_effects=True),
    )(
        band_rows,
        jnp.transpose(filter_bands, (1, 0, 2)),
        background.reshape(256, 256),
        scale_x.reshape(128, 256),
        scale_y.reshape(128, 256),
    )
    return inc.reshape(background.shape), bf.reshape(2, 16, CAP, LANES)


def solution(mesh):
    strips = P(None, None, ("lon", "band"), None)
    faces = P(None, ("lon", "band"), None)
    return jax.shard_map(
        shards,
        mesh=mesh,
        in_specs=(strips, faces, faces, P(), P()),
        out_specs=(strips, P(None, None, "band", "lon")),
        check_vma=False,
    )
```

time: 348 us -> 35.1 us (0.10); the launches traced: 343 us -> 34.5 us
  local copies, waits for them, and re-layouts: 186 us -> 2.52 us
  other arithmetic: 47.4 us -> 0 us
  starting transfers between devices: 42 us -> 0 us
  waiting for transfers between devices: 36.5 us -> 0 us
  Pallas kernels: 0 us -> 31.4 us
  loops' own time: 27.8 us -> 0 us
  between operations: 4.14 us -> 0.65 us
    dynamic_update_slice x20 -> x0, local copies, waits for them, and re-layouts: 103 us -> none  [the longest x16 73 us: add_band(): lax.dynamic_update_slice_in_dim(whole, current + arrived[index], starts[i...]
    slice x52 -> x0, local copies, waits for them, and re-layouts: 38.1 us -> none  [the longest x4 8.08 us: band_margin(): edges = jnp.concatenate([wide[:, :depth], lower], 1)]
    pallas_call x0 -> x1, Pallas kernels: none -> 31.4 us  [shards(): pl.pallas_call(kernel, out_shape=(jax.ShapeDtypeStruct((256, 256), f32),...]
    another operation x1 -> x0, loops' own time: 27.8 us -> none  [place_rows(): whole = lax.fori_loop(0, count, add_band, empty)]
    all_to_all x2 -> x0, waiting for transfers between devices: 23.1 us -> none  [the longest x1 14.4 us: shards(): lax.all_to_all(sent, 'band', split_axis=0, concat_axis=0, tiled=True)]
    ppermute x12 -> x0, starting transfers between devices: 22.4 us -> none  [the longest x6 13.1 us: extended(): lax.ppermute(lax.slice_in_dim(block, 0, width, axis=dim), axis, backward)]
    all_to_all x2 -> x0, starting transfers between devices: 19.6 us -> none  [the longest x1 11.3 us: shards(): lax.all_to_all(outgoing, 'band', split_axis=0, concat_axis=0, tiled=True)]
    dynamic_slice x19 -> x0, local copies, waits for them, and re-layouts: 15.5 us -> none  [the longest x16 9.25 us: add_band(): current = lax.dynamic_slice_in_dim(whole, starts[index], height, 2)]
  transfers between devices with their start and end apart: 14 -> 0, of which waited for: 6 -> 0; matrix products, arithmetic and copies ran while one was open for 14% -> 0% of each run, Pallas kernels for 0% -> 0%
where the time goes in v1:
time: 35.1 us; the launch traced here: 34.5 us
  Pallas kernels  31.4 us (89%)
  local copies, waits for them, and re-layouts  2.52 us (7%)
  between operations  0.65 us (2%)
    pallas_call x1, Pallas kernels, shards(): pl.pallas_call(kernel, out_shape=(jax.ShapeDtypeStruct((256, 256), f32),...  31.4 us
    unnamed x4, local copies, waits for them, and re-layouts  2.52 us

profile of v1, /device:TPU:0, one launch (start us, length us, event | category | flops | bytes accessed | tf_op | source)
XLA Modules:
  0.0 34.5 jit_solution(6268078055409670101)
XLA Ops:
  0.6 31.4 %shard_map.68 = (f32[256,256]{1,0:T(8,128)}, f32[1024,128]{1,0:T(8,128)}) custom-call(s32[16]{0:T(128)} %rows_ref.1, f32[5,2,16]{2,1,0:T(2,128)} %bitcast.11, f32[256,256]{1,0:T(8,128)} %bitcast.7, f32[128,256]{1,0:T(8,128)} %bitcast.9, f32[128,256]{1,0:T(8,128)} %bitcast.10), custom_call_target="tpu_custom_call" | custom-call | tf_op jit(solution)/shard_map/pallas_call | solution.py:298
  32.0 0.0 copy-start
  32.0 1.7 %copy.9 = f32[2,16,8,256]{3,2,1,0:T(8,128)} copy(f32[2,16,8,256]{3,2,1,0:T(8,128)} %bitcast.8) | data formatting | bytes 524288
  33.7 0.0 copy-done
  33.7 0.8 %copy.10 = f32[2,16,32,128]{3,2,1,0:T(8,128)} copy(f32[2,16,32,128]{3,2,1,0:T(8,128)S(1)} %bitcast.6) | data formatting | bytes 1048576
Async XLA Ops:
  32.0 1.7 %copy-start = (f32[1024,128]{1,0:T(8,128)S(1)}, f32[1024,128]{1,0:T(8,128)}, u32[]{:S(2)}) copy-start(f32[1024,128]{1,0:T(8,128)} %get-tuple-element.5) | copy-start | bytes 1572868

commit v2 on v1

v2 whole, which is shorter than its diff:
```python
import functools

import jax
import jax.numpy as jnp
from jax import lax
from jax.experimental import pallas as pl
from jax.experimental.pallas import tpu as pltpu
from jax.sharding import PartitionSpec as P

MESH = pl.DeviceIdType.MESH
STEPS = 8
CAP = 32
DEPTH = 8
ROUNDS = STEPS // DEPTH
WIDTH = 8
LANES = 128
SX, SY = 2, 3


def roll(x, shift):
    return pltpu.roll(x, shift, x.ndim - 1)


def diffuse(get_field, get_sx, get_sy, put, lane):
    last, first = lane == LANES - 1, lane == 0
    held = [None] * DEPTH
    flux = [None] * DEPTH

    def push(step, column, field):
        if step == DEPTH:
            put(column, field)
            return
        before, west = held[step], flux[step]
        held[step] = field
        if before is None:
            return
        p = column - 1
        sx = get_sx(p)
        east = [sx[i] * (field[i] - before[i]) for i in range(2)]
        flux[step] = east
        if west is None:
            return
        sy = get_sy(p)
        ra, rb = roll(before[0], LANES - 1), roll(before[1], LANES - 1)
        up = [jnp.where(last, rb, ra), rb]
        north = [sy[i] * (up[i] - before[i]) for i in range(2)]
        qa, qb = roll(north[0], 1), roll(north[1], 1)
        south = [jnp.where(first, qb, qa), jnp.where(first, qa, qb)]
        new = [before[i] + east[i] - west[i] + north[i] - south[i] for i in range(2)]
        push(step + 1, p, new)

    for column in range(-DEPTH, WIDTH + DEPTH):
        push(0, column, get_field(column))


def torus(band):
    z, y = band // 4, lax.rem(band, 4)
    return [
        lax.rem(z + 1, 4) * 4 + y,
        lax.rem(z + 3, 4) * 4 + y,
        z * 4 + lax.rem(y + 1, 4),
        z * 4 + lax.rem(y + 3, 4),
    ]


def strips_kernel(
    rows_ref, bg_ref, sx_ref, sy_ref,
    win_ref, nat_ref,
    raw_bg, raw_sx, raw_sy, own, halo0, halo1, mid, done, send_buf, rows, st,
    near_sem, in_sem, hs_sem, hr_sem, as_sem, ar_sem,
):
    n_band, n_lon = lax.axis_size("band"), lax.axis_size("lon")
    band, lon = lax.axis_index("band"), lax.axis_index("lon")
    at_end, at_start = band == n_band - 1, band == 0
    right = (
        jnp.where(at_end, 0, band + 1),
        jnp.where(at_end, lax.rem(lon + 1, n_lon), lon),
    )
    left = (
        jnp.where(at_start, n_band - 1, band - 1),
        jnp.where(at_start, lax.rem(lon + n_lon - 1, n_lon), lon),
    )
    near = [(b, lon) for b in torus(band)]

    barrier = pltpu.get_barrier_semaphore()
    for side in [left, right] + near:
        pl.semaphore_signal(barrier, inc=1, device_id=side, device_id_type=MESH)

    copies = []
    for ref, raw in ((bg_ref, raw_bg), (sx_ref, raw_sx), (sy_ref, raw_sy)):
        for half in range(2):
            copies.append(
                pltpu.make_async_copy(
                    ref.at[:, pl.ds(half * LANES, LANES)],
                    raw.at[half],
                    in_sem.at[len(copies)],
                )
            )
    copies.append(pltpu.make_async_copy(rows_ref, rows, in_sem.at[len(copies)]))
    for copy in copies:
        copy.start()

    lane = lax.broadcasted_iota(jnp.int32, (8, LANES), 1)
    for copy in copies:
        copy.wait()
    for h in range(2):
        for c in range(WIDTH):
            for half in range(2):
                for v in range(2):
                    own[h, c, v, half] = raw_bg[half, pl.ds(v * 128 + h * 64 + c, 8, stride=8), :]
                own[h, c, SX, half] = raw_sx[half, pl.ds(h * 64 + c, 8, stride=8), :]
                face = raw_sy[half, pl.ds(h * 64 + c, 8, stride=8), :]
                if half == 1:
                    face = jnp.where(lane == LANES - 1, 0.0, face)
                own[h, c, SY, half] = face

    pl.semaphore_wait(barrier, 6)

    def halo_copies(r, h):
        src, dst = ((own, halo0), (mid, halo1))[r]
        return [
            pltpu.make_async_remote_copy(
                src_ref=src.at[h, pl.ds(0, DEPTH)],
                dst_ref=dst.at[h, 1],
                send_sem=hs_sem.at[r, h, 0],
                recv_sem=hr_sem.at[r, h, 1],
                device_id=left,
                device_id_type=MESH,
            ),
            pltpu.make_async_remote_copy(
                src_ref=src.at[h, pl.ds(WIDTH - DEPTH, DEPTH)],
                dst_ref=dst.at[h, 0],
                send_sem=hs_sem.at[r, h, 1],
                recv_sem=hr_sem.at[r, h, 0],
                device_id=right,
                device_id_type=MESH,
            ),
        ]

    for h in range(2):
        for copy in halo_copies(0, h):
            copy.start()

    for hop in range(3):
        for peer in near:
            pl.semaphore_signal(
                near_sem.at[hop], inc=1, device_id=peer, device_id_type=MESH
            )
        pl.semaphore_wait(near_sem.at[hop], 4)

    total = jnp.int32(0)
    for b in range(16):
        st[b] = total
        total = total + rows[b]

    def one_round(r, h):
        inner, halo = ((own, halo0), (mid, halo1))[r]

        def pick(mine, side, column, unit):
            if column < 0:
                at = (h, 0, column + DEPTH)
                ref = side
            elif column < WIDTH:
                at = (h, column)
                ref = mine
            else:
                at = (h, 1, column - WIDTH)
                ref = side
            return [ref[at + (unit, half)] for half in range(2)]

        def put(column, new):
            if r + 1 < ROUNDS:
                for half in range(2):
                    mid[h, column, :, half] = new[half]
                return
            for half in range(2):
                done[h, column, :, half] = new[half]
                for v in range(2):
                    nat_ref[half, pl.ds(v * 128 + h * 64 + column, 8, stride=8), :] = new[half][v]

        diffuse(
            lambda column: pick(inner, halo, column, slice(0, 2)),
            lambda column: pick(own, halo0, column, SX),
            lambda column: pick(own, halo0, column, SY),
            put,
            lane,
        )

    for r in range(ROUNDS):
        for h in range(2):
            for copy in halo_copies(r, h):
                copy.wait_recv()
            one_round(r, h)
            if r + 1 < ROUNDS:
                for copy in halo_copies(r + 1, h):
                    copy.start()

    def slot(b):
        return win_ref.at[pl.ds(pl.multiple_of(b * 64, 64), 64)]

    def target(i):
        return i // 4 * 4 + lax.rem(lax.rem(band, 4) + lax.rem(i, 4), 4)

    def band_copy(i):
        return pltpu.make_async_remote_copy(
            src_ref=send_buf.at[i],
            dst_ref=slot(band),
            send_sem=as_sem.at[i],
            recv_sem=ar_sem.at[band],
            device_id=(target(i), lon),
            device_id_type=MESH,
        )

    def send(i, carry):
        b = target(i)
        start = st[b]
        for c in range(WIDTH):
            parts = []
            for q in range(4):
                v, h = q // 2, q % 2
                x = jnp.where(lane >= start, done[h, c, v, 0], done[h, c, v, 1])
                parts.append(roll(x, (32 * q + 256 - start) & 127))
            send_buf[i, pl.ds(c * 8, 8), :] = jnp.where(
                lane < 64,
                jnp.where(lane < 32, parts[0], parts[1]),
                jnp.where(lane < 96, parts[2], parts[3]),
            )

        @pl.when(b != band)
        def _():
            band_copy(i).start()

        @pl.when(b == band)
        def _():
            pltpu.make_async_copy(send_buf.at[i], slot(band), ar_sem.at[band]).start()

        return carry

    lax.fori_loop(0, n_band, send, 0)

    for r in range(ROUNDS):
        for h in range(2):
            for copy in halo_copies(r, h):
                copy.wait_send()

    def arrive(b, carry):
        pltpu.make_async_copy(send_buf.at[0], slot(b), ar_sem.at[b]).wait()
        return carry

    lax.fori_loop(0, n_band, arrive, 0)

    def sent(i, carry):
        @pl.when(target(i) != band)
        def _():
            band_copy(i).wait_send()

        return carry

    lax.fori_loop(0, n_band, sent, 0)


def filter_kernel(
    rows_ref, filt_ref, win_ref, nat_ref, inc_ref, bf_ref,
    rows, filt, band_nat, out_inc, out_bf, in_sem, out_sem,
):
    scalars = [
        pltpu.make_async_copy(rows_ref, rows, in_sem.at[0]),
        pltpu.make_async_copy(filt_ref, filt, in_sem.at[1]),
    ]
    for copy in scalars:
        copy.start()
    for s in range(8):
        flat = win_ref[pl.ds(s, LANES, stride=8), :].T
        for q in range(4):
            v, h = q // 2, q % 2
            band_nat[v, h * 8 + s] = flat[q * CAP:(q + 1) * CAP, :]
    for copy in scalars:
        copy.wait()

    inside = lax.broadcasted_iota(jnp.int32, (CAP, LANES), 0) < rows[lax.axis_index("band")]
    outs = []
    for v in range(2):
        for level in range(16):
            value = band_nat[v, level]
            for o in range(5):
                if 0 <= level + o - 2 < 16:
                    value = value + filt[o, v, level] * band_nat[v, level + o - 2]
            at = (v * 16 + level) * CAP
            out_bf[at:at + CAP, :] = jnp.where(inside, value, 0.0)
        outs.append(
            pltpu.make_async_copy(
                out_bf.at[pl.ds(v * 512, 512)], bf_ref.at[pl.ds(v * 512, 512)], out_sem.at[v]
            )
        )
        outs[-1].start()

    for v in range(2):
        for level in range(16):
            for half in range(2):
                at = v * 128 + level * 8
                value = nat_ref[half, at:at + 8, :]
                for o in range(5):
                    if 0 <= level + o - 2 < 16:
                        beside = at + (o - 2) * 8
                        value = value + filt[o, v, level] * nat_ref[half, beside:beside + 8, :]
                out_inc[at:at + 8, half * LANES:(half + 1) * LANES] = value
    outs.append(pltpu.make_async_copy(out_inc, inc_ref, out_sem.at[2]))
    outs[-1].start()
    for copy in outs:
        copy.wait()


def shards(background, scale_x, scale_y, filter_bands, band_rows):
    f32 = jnp.float32
    any_space = pl.BlockSpec(memory_space=pl.ANY)
    hbm = pl.BlockSpec(memory_space=pltpu.HBM)
    resident = pl.BlockSpec(memory_space=pltpu.VMEM)
    vmem = pltpu.VMEM
    dma = pltpu.SemaphoreType.DMA
    win, nat = pl.pallas_call(
        strips_kernel,
        out_shape=(
            jax.ShapeDtypeStruct((1024, LANES), f32),
            jax.ShapeDtypeStruct((2, 256, LANES), f32),
        ),
        in_specs=[any_space, hbm, hbm, hbm],
        out_specs=(resident, resident),
        scratch_shapes=[
            vmem((2, 256, LANES), f32),
            vmem((2, 128, LANES), f32),
            vmem((2, 128, LANES), f32),
            vmem((2, WIDTH, 4, 2, 8, LANES), f32),
            vmem((2, 2, DEPTH, 4, 2, 8, LANES), f32),
            vmem((2, 2, DEPTH, 2, 2, 8, LANES), f32),
            vmem((2, WIDTH, 2, 2, 8, LANES), f32),
            vmem((2, WIDTH, 2, 2, 8, LANES), f32),
            vmem((16, 64, LANES), f32),
            pltpu.SMEM((16,), jnp.int32),
            pltpu.SMEM((16,), jnp.int32),
            pltpu.SemaphoreType.REGULAR((3,)),
            dma((7,)),
            dma((ROUNDS, 2, 2)),
            dma((ROUNDS, 2, 2)),
            dma((16,)),
            dma((16,)),
        ],
        compiler_params=pltpu.CompilerParams(
            collective_id=0, has_side_effects=True, vmem_limit_bytes=16 << 20
        ),
    )(
        pltpu.with_memory_space_constraint(band_rows, pltpu.HBM),
        pltpu.with_memory_space_constraint(background.reshape(256, 256), pltpu.HBM),
        pltpu.with_memory_space_constraint(scale_x.reshape(128, 256), pltpu.HBM),
        pltpu.with_memory_space_constraint(scale_y.reshape(128, 256), pltpu.HBM),
    )
    inc, bf = pl.pallas_call(
        filter_kernel,
        out_shape=(
            jax.ShapeDtypeStruct((256, 256), f32),
            jax.ShapeDtypeStruct((1024, LANES), f32),
        ),
        in_specs=[any_space, any_space, resident, resident],
        out_specs=(hbm, hbm),
        scratch_shapes=[
            pltpu.SMEM((16,), jnp.int32),
            pltpu.SMEM((5, 2, 16), f32),
            vmem((2, 16, CAP, LANES), f32),
            vmem((256, 256), f32),
            vmem((1024, LANES), f32),
            dma((2,)),
            dma((3,)),
        ],
        compiler_params=pltpu.CompilerParams(vmem_limit_bytes=16 << 20),
    )(band_rows, jnp.transpose(filter_bands, (1, 0, 2)), win, nat)
    return inc.reshape(background.shape), bf.reshape(2, 16, CAP, LANES)


def solution(mesh):
    strips = P(None, None, ("lon", "band"), None)
    faces = P(None, ("lon", "band"), None)
    return jax.shard_map(
        shards,
        mesh=mesh,
        in_specs=(strips, faces, faces, P(), P()),
        out_specs=(strips, P(None, None, "band", "lon")),
        check_vma=False,
    )
```

time: 35.1 us -> 32.7 us (0.932)
  local copies, waits for them, and re-layouts: 2.52 us -> 0.64 us
    unnamed x4, local copies, waits for them, and re-layouts: 2.52 us -> 0.64 us
    pallas_call x1 -> x2, Pallas kernels: 31.4 us -> 31.1 us  [the longest x1 29.4 us: shards(): pl.pallas_call(strips_kernel, out_shape=(jax.ShapeDtypeStruct((1024, LANE...]
where the time goes in v2:
time: 32.7 us; the launch traced here: 32.4 us
  Pallas kernels  31.1 us (95%)
  between operations  0.66 us (2%)
  local copies, waits for them, and re-layouts  0.64 us (2%)
    pallas_call x1, Pallas kernels, shards(): pl.pallas_call(strips_kernel, out_shape=(jax.ShapeDtypeStruct((1024, LANE...  29.4 us
    pallas_call x1, Pallas kernels, shards(): pl.pallas_call(filter_kernel, out_shape=(jax.ShapeDtypeStruct((256, 256),...  1.79 us

profile of v2, /device:TPU:0, one launch (start us, length us, event | category | flops | bytes accessed | tf_op | source)
XLA Modules:
  0.0 32.4 jit_solution(2616011206992874069)
XLA Ops:
  0.6 0.0 copy-start
  0.6 29.4 %shard_map.68 = (f32[1024,128]{1,0:T(8,128)S(1)}, f32[2,256,128]{2,1,0:T(8,128)S(1)}) custom-call(s32[16]{0:T(128)} %rows_ref.3, f32[256,256]{1,0:T(8,128)} %bitcast.7, f32[128,256]{1,0:T(8,128)} %bitcast.8, f32[128,256]{1,0:T(8,128)} %bitcast.9), custom_call_target="tpu_custom_call" | custom-call | tf_op jit(solution)/shard_map/pallas_call | solution.py:320
  30.0 0.0 copy-start.1
  30.0 0.0 copy-done
  30.0 0.6 %copy-done.1 = s32[16]{0:T(128)S(1)} copy-done((s32[16]{0:T(128)S(1)}, s32[16]{0:T(128)}, u32[]{:S(2)}) %copy-start.1) | copy-done | bytes 88
  30.7 1.8 %shard_map.69 = (f32[256,256]{1,0:T(8,128)}, f32[1024,128]{1,0:T(8,128)}) custom-call(s32[16]{0:T(128)S(1)} %copy-done.1, f32[5,2,16]{2,1,0:T(2,128)S(1)} %bitcast.6, f32[1024,128]{1,0:T(8,128)S(1)} %get-tuple-element.6.win_ref, f32[2,256,128]{2,1,0:T(8,128)S(1)} %get-tuple-element.7.nat_ref), custom_call_target="tpu_custom_call" | custom-call | tf_op jit(solution)/shard_map/pallas_call | solution.py:356
Async XLA Ops:
  0.6 29.4 %copy-start = (f32[2,5,16]{2,0,1:T(2,128)S(1)}, f32[2,5,16]{2,0,1:T(2,128)}, u32[]{:S(2)}) copy-start(f32[2,5,16]{2,0,1:T(2,128)} %param.8) | copy-start | bytes 1924
  30.0 0.7 %copy-start.1 = (s32[16]{0:T(128)S(1)}, s32[16]{0:T(128)}, u32[]{:S(2)}) copy-start(s32[16]{0:T(128)} %rows_ref.3) | copy-start | bytes 196

commit v3 on v2

v3 whole, which is shorter than its diff:
```python
import jax
import jax.numpy as jnp
from jax import lax
from jax.experimental import pallas as pl
from jax.experimental.pallas import tpu as pltpu
from jax.sharding import PartitionSpec as P

MESH = pl.DeviceIdType.MESH
STEPS = 8
CAP = 32
WIDTH = 8
LANES = 128
LEFT, OWN, RIGHT = 0, 1, 2
SX, SY, VAR = 0, 1, 2


def roll(x, shift):
    return pltpu.roll(x, shift, x.ndim - 1)


def diffuse(get_field, get_sx, get_sy, put, lane):
    last, first = lane == LANES - 1, lane == 0
    held = [None] * STEPS
    flux = [None] * STEPS

    def push(step, column, field):
        if step == STEPS:
            put(column, field)
            return
        before, west = held[step], flux[step]
        held[step] = field
        if before is None:
            return
        p = column - 1
        sx = get_sx(p)
        east = [sx[i] * (field[i] - before[i]) for i in range(2)]
        flux[step] = east
        if west is None:
            return
        sy = get_sy(p)
        ra, rb = roll(before[0], LANES - 1), roll(before[1], LANES - 1)
        up = [jnp.where(last, rb, ra), rb]
        north = [sy[i] * (up[i] - before[i]) for i in range(2)]
        qa, qb = roll(north[0], 1), roll(north[1], 1)
        south = [jnp.where(first, qb, qa), jnp.where(first, qa, qb)]
        new = [before[i] + east[i] - west[i] + north[i] - south[i] for i in range(2)]
        push(step + 1, p, new)

    for column in range(-STEPS, WIDTH + STEPS):
        push(0, column, get_field(column))


def torus(band):
    z, y = band // 4, lax.rem(band, 4)
    return [
        lax.rem(z + 1, 4) * 4 + y,
        lax.rem(z + 3, 4) * 4 + y,
        z * 4 + lax.rem(y + 1, 4),
        z * 4 + lax.rem(y + 3, 4),
    ]


def strips_kernel(
    rows_ref, filt_ref, bg_ref, sx_ref, sy_ref,
    win_ref, inc_ref,
    raw, cols, done, nat, send_buf, rows, filt, st,
    near_sem, in_sem, hs_sem, hr_sem, as_sem, ar_sem,
):
    n_band, n_lon = lax.axis_size("band"), lax.axis_size("lon")
    band, lon = lax.axis_index("band"), lax.axis_index("lon")
    at_end, at_start = band == n_band - 1, band == 0
    right = (
        jnp.where(at_end, 0, band + 1),
        jnp.where(at_end, lax.rem(lon + 1, n_lon), lon),
    )
    left = (
        jnp.where(at_start, n_band - 1, band - 1),
        jnp.where(at_start, lax.rem(lon + n_lon - 1, n_lon), lon),
    )
    near = [(b, lon) for b in torus(band)]

    barrier = pltpu.get_barrier_semaphore()
    for side in [left, right] + near:
        pl.semaphore_signal(barrier, inc=1, device_id=side, device_id_type=MESH)

    copies = [
        pltpu.make_async_copy(sx_ref, raw.at[SX], in_sem.at[0]),
        pltpu.make_async_copy(sy_ref, raw.at[SY], in_sem.at[1]),
        pltpu.make_async_copy(bg_ref, raw.at[pl.ds(VAR, 2)], in_sem.at[2]),
    ]
    scalars = [
        pltpu.make_async_copy(rows_ref, rows, in_sem.at[3]),
        pltpu.make_async_copy(filt_ref, filt, in_sem.at[4]),
    ]
    for copy in copies + scalars:
        copy.start()

    def halo_copy(h, i, unit):
        device, strip = ((left, RIGHT), (right, LEFT))[i]
        first, count = 0, WIDTH
        if i == 0 and unit in (SX, SY):
            count = WIDTH - 1
        elif i == 1 and unit == SY:
            first, count = 1, WIDTH - 1
        return pltpu.make_async_remote_copy(
            src_ref=cols.at[OWN, h, unit, pl.ds(first, count)],
            dst_ref=cols.at[strip, h, unit, pl.ds(first, count)],
            send_sem=hs_sem.at[h, i, unit],
            recv_sem=hr_sem.at[h, i, unit],
            device_id=device,
            device_id_type=MESH,
        )

    lane = lax.broadcasted_iota(jnp.int32, (8, LANES), 1)
    for h in range(2):
        for unit in range(4):
            if h == 0 and unit < 3:
                copies[unit].wait()
            for c in range(WIDTH):
                for half in range(2):
                    tile = raw[unit, h, pl.ds(half * 8 + c, 8, stride=16), :]
                    if unit == SY and half == 1:
                        tile = jnp.where(lane == LANES - 1, 0.0, tile)
                    cols[OWN, h, unit, c, half] = tile
        if h == 0:
            pl.semaphore_wait(barrier, 6)
        for unit in range(4):
            for i in range(2):
                halo_copy(h, i, unit).start()

    for hop in range(3):
        for peer in near:
            pl.semaphore_signal(
                near_sem.at[hop], inc=1, device_id=peer, device_id_type=MESH
            )
        pl.semaphore_wait(near_sem.at[hop], 4)

    for copy in scalars:
        copy.wait()
    total = jnp.int32(0)
    for b in range(16):
        st[b] = total
        total = total + rows[b]

    def run_block(h, v):
        def load(unit, column):
            strip, c = (column + WIDTH) // WIDTH, (column + WIDTH) % WIDTH
            return [cols[strip, h, unit, c, half] for half in range(2)]

        def put(column, new):
            for half in range(2):
                done[h, column, v, half] = new[half]
                row = ((v * 16 + h * 8) * 2 + half) * 8 + column
                nat[pl.ds(row, 8, stride=16), :] = new[half]

        diffuse(
            lambda column: load(VAR + v, column),
            lambda column: load(SX, column),
            lambda column: load(SY, column),
            put,
            lane,
        )

    for h in range(2):
        for unit in range(4):
            for i in range(2):
                halo_copy(h, i, unit).wait_recv()
            if unit >= VAR:
                run_block(h, unit - VAR)

    def slot(b):
        return win_ref.at[pl.ds(pl.multiple_of(b * 64, 64), 64)]

    def target(i):
        return i // 4 * 4 + lax.rem(lax.rem(band, 4) + lax.rem(i, 4), 4)

    def band_copy(i):
        return pltpu.make_async_remote_copy(
            src_ref=send_buf.at[i],
            dst_ref=slot(band),
            send_sem=as_sem.at[i],
            recv_sem=ar_sem.at[band],
            device_id=(target(i), lon),
            device_id_type=MESH,
        )

    def send(i, carry):
        b = target(i)
        start = st[b]
        for c in range(WIDTH):
            parts = []
            for q in range(4):
                v, h = q // 2, q % 2
                x = jnp.where(lane >= start, done[h, c, v, 0], done[h, c, v, 1])
                parts.append(roll(x, (32 * q + 256 - start) & 127))
            send_buf[i, pl.ds(c * 8, 8), :] = jnp.where(
                lane < 64,
                jnp.where(lane < 32, parts[0], parts[1]),
                jnp.where(lane < 96, parts[2], parts[3]),
            )

        @pl.when(b != band)
        def _():
            band_copy(i).start()

        @pl.when(b == band)
        def _():
            pltpu.make_async_copy(send_buf.at[i], slot(band), ar_sem.at[band]).start()

        return carry

    lax.fori_loop(0, n_band, send, 0)

    for v in range(2):
        for level in range(16):
            at = (v * 16 + level) * 16
            value = nat[at:at + 16, :]
            for o in range(5):
                if 0 <= level + o - 2 < 16:
                    beside = at + (o - 2) * 16
                    value = value + filt[o, v, level] * nat[beside:beside + 16, :]
            inc_ref[at:at + 16, :] = value

    for h in range(2):
        for unit in range(4):
            for i in range(2):
                halo_copy(h, i, unit).wait_send()

    def sent(i, carry):
        @pl.when(target(i) != band)
        def _():
            band_copy(i).wait_send()

        return carry

    def arrive(b, carry):
        pltpu.make_async_copy(send_buf.at[0], slot(b), ar_sem.at[b]).wait()
        return carry

    lax.fori_loop(0, n_band, sent, 0)
    lax.fori_loop(0, n_band, arrive, 0)


def filter_kernel(
    rows_ref, filt_ref, win_ref, inc_ref, out_inc_ref, bf_ref,
    rows, filt, band_nat, out_bf, in_sem, out_sem,
):
    outs = [pltpu.make_async_copy(inc_ref, out_inc_ref, out_sem.at[2])]
    scalars = [
        pltpu.make_async_copy(rows_ref, rows, in_sem.at[0]),
        pltpu.make_async_copy(filt_ref, filt, in_sem.at[1]),
    ]
    for copy in scalars + outs:
        copy.start()
    for s in range(8):
        flat = win_ref[pl.ds(s, LANES, stride=8), :].T
        for q in range(4):
            v, h = q // 2, q % 2
            band_nat[v, h * 8 + s] = flat[q * CAP:(q + 1) * CAP, :]
    for copy in scalars:
        copy.wait()

    inside = lax.broadcasted_iota(jnp.int32, (CAP, LANES), 0) < rows[lax.axis_index("band")]
    for v in range(2):
        for level in range(16):
            value = band_nat[v, level]
            for o in range(5):
                if 0 <= level + o - 2 < 16:
                    value = value + filt[o, v, level] * band_nat[v, level + o - 2]
            at = (v * 16 + level) * CAP
            out_bf[at:at + CAP, :] = jnp.where(inside, value, 0.0)
        outs.append(
            pltpu.make_async_copy(
                out_bf.at[pl.ds(v * 512, 512)], bf_ref.at[pl.ds(v * 512, 512)], out_sem.at[v]
            )
        )
        outs[-1].start()
    for copy in outs:
        copy.wait()


def tiles(a):
    n = a.size // 2048
    return jnp.transpose(a.reshape(n, 8, 2, LANES), (0, 2, 1, 3)).reshape(n * 16, LANES)


def shards(background, scale_x, scale_y, filter_bands, band_rows):
    f32 = jnp.float32
    any_space = pl.BlockSpec(memory_space=pl.ANY)
    hbm = pl.BlockSpec(memory_space=pltpu.HBM)
    resident = pl.BlockSpec(memory_space=pltpu.VMEM)
    vmem = pltpu.VMEM
    dma = pltpu.SemaphoreType.DMA

    def stay(a):
        return pltpu.with_memory_space_constraint(a, pltpu.HBM)

    filters = jnp.transpose(filter_bands, (1, 0, 2))
    win, inc = pl.pallas_call(
        strips_kernel,
        out_shape=(
            jax.ShapeDtypeStruct((1024, LANES), f32),
            jax.ShapeDtypeStruct((512, LANES), f32),
        ),
        in_specs=[hbm] * 5,
        out_specs=(resident, resident),
        scratch_shapes=[
            vmem((4, 2, 128, LANES), f32),
            vmem((3, 2, 4, WIDTH, 2, 8, LANES), f32),
            vmem((2, WIDTH, 2, 2, 8, LANES), f32),
            vmem((512, LANES), f32),
            vmem((16, 64, LANES), f32),
            pltpu.SMEM((16,), jnp.int32),
            pltpu.SMEM((5, 2, 16), f32),
            pltpu.SMEM((16,), jnp.int32),
            pltpu.SemaphoreType.REGULAR((3,)),
            dma((5,)),
            dma((2, 2, 4)),
            dma((2, 2, 4)),
            dma((16,)),
            dma((16,)),
        ],
        compiler_params=pltpu.CompilerParams(
            collective_id=0, has_side_effects=True, vmem_limit_bytes=16 << 20
        ),
    )(
        stay(band_rows),
        stay(filters),
        stay(tiles(background).reshape(2, 2, 128, LANES)),
        stay(tiles(scale_x).reshape(2, 128, LANES)),
        stay(tiles(scale_y).reshape(2, 128, LANES)),
    )
    inc, bf = pl.pallas_call(
        filter_kernel,
        out_shape=(
            jax.ShapeDtypeStruct((512, LANES), f32),
            jax.ShapeDtypeStruct((1024, LANES), f32),
        ),
        in_specs=[any_space, any_space, resident, resident],
        out_specs=(hbm, hbm),
        scratch_shapes=[
            pltpu.SMEM((16,), jnp.int32),
            pltpu.SMEM((5, 2, 16), f32),
            vmem((2, 16, CAP, LANES), f32),
            vmem((1024, LANES), f32),
            dma((2,)),
            dma((3,)),
        ],
        compiler_params=pltpu.CompilerParams(vmem_limit_bytes=16 << 20),
    )(band_rows, filters, win, inc)
    inc = jnp.transpose(inc.reshape(32, 2, 8, LANES), (0, 2, 1, 3))
    return inc.reshape(background.shape), bf.reshape(2, 16, CAP, LANES)


def solution(mesh):
    strips = P(None, None, ("lon", "band"), None)
    faces = P(None, ("lon", "band"), None)
    return jax.shard_map(
        shards,
        mesh=mesh,
        in_specs=(strips, faces, faces, P(), P()),
        out_specs=(strips, P(None, None, "band", "lon")),
        check_vma=False,
    )
```

time: 32.7 us -> 31.6 us (0.966)
  Pallas kernels: 31.1 us -> 30.1 us
    pallas_call x1, Pallas kernels: 29.4 us -> 28.4 us  [shards(): pl.pallas_call(strips_kernel, out_shape=(jax.ShapeDtypeStruct((1024, LANE...]
where the time goes in v3:
time: 31.6 us; the launch traced here: 31.4 us
  Pallas kernels  30.1 us (95%)
  between operations  0.66 us (2%)
  local copies, waits for them, and re-layouts  0.64 us (2%)
    pallas_call x1, Pallas kernels, shards(): pl.pallas_call(strips_kernel, out_shape=(jax.ShapeDtypeStruct((1024, LANE...  28.4 us
    pallas_call x1, Pallas kernels, shards(): pl.pallas_call(filter_kernel, out_shape=(jax.ShapeDtypeStruct((512, LANES...  1.69 us
    unnamed x4, local copies, waits for them, and re-layouts  0.64 us

profile of v3, /device:TPU:0, one launch (start us, length us, event | category | flops | bytes accessed | tf_op | source)
XLA Modules:
  0.0 31.4 jit_solution(16392265539715938417)
XLA Ops:
  0.6 0.0 copy-start
  0.6 28.4 %shard_map.68 = (f32[1024,128]{1,0:T(8,128)S(1)}, f32[512,128]{1,0:T(8,128)S(1)}) custom-call(s32[16]{0:T(128)} %rows_ref.3, f32[5,2,16]{2,1,0:T(2,128)} %bitcast.22, f32[2,2,128,128]{3,2,1,0:T(8,128)} %bitcast.24, f32[2,128,128]{2,1,0:T(8,128)} %bitcast.25, f32[2,128,128]{2,1,0:T(8,128)} %bitcast.26), custom_call_target="tpu_custom_call" | custom-call | tf_op jit(solution)/shard_map/pallas_call | solution.py:299
  29.1 0.0 copy-start.1
  29.1 0.0 copy-done
  29.1 0.6 %copy-done.1 = s32[16]{0:T(128)S(1)} copy-done((s32[16]{0:T(128)S(1)}, s32[16]{0:T(128)}, u32[]{:S(2)}) %copy-start.1) | copy-done | bytes 88
  29.8 1.7 %shard_map.69 = (f32[512,128]{1,0:T(8,128)}, f32[1024,128]{1,0:T(8,128)}) custom-call(s32[16]{0:T(128)S(1)} %copy-done.1, f32[5,2,16]{2,1,0:T(2,128)S(1)} %bitcast.23, f32[1024,128]{1,0:T(8,128)S(1)} %get-tuple-element.6.win_ref, f32[512,128]{1,0:T(8,128)S(1)} %get-tuple-element.7.inc_ref), custom_call_target="tpu_custom_call" | custom-call | tf_op jit(solution)/shard_map/pallas_call | solution.py:333
Async XLA Ops:
  0.6 28.5 %copy-start = (f32[2,5,16]{2,0,1:T(2,128)S(1)}, f32[2,5,16]{2,0,1:T(2,128)}, u32[]{:S(2)}) copy-start(f32[2,5,16]{2,0,1:T(2,128)} %param.8) | copy-start | bytes 1924
  29.1 0.7 %copy-start.1 = (s32[16]{0:T(128)S(1)}, s32[16]{0:T(128)}, u32[]{:S(2)}) copy-start(s32[16]{0:T(128)} %rows_ref.3) | copy-start | bytes 196

commit v4 on v3

--- a/solution.py
+++ b/solution.py
@@ -149,12 +149,20 @@
 
         def put(column, new):
             for half in range(2):
-                done[h, column, v, half] = new[half]
+                turn = 32 * (2 * v + h)
+                done[column, 2 * v + h, half] = roll(new[half], turn) if turn else new[half]
                 row = ((v * 16 + h * 8) * 2 + half) * 8 + column
                 nat[pl.ds(row, 8, stride=16), :] = new[half]
 
+        def get_field(column):
+            if column == -WIDTH:
+                for i in range(2):
+                    for unit in ((SX, SY, VAR), (VAR + 1,))[v]:
+                        halo_copy(h, i, unit).wait_recv()
+            return load(VAR + v, column)
+
         diffuse(
-            lambda column: load(VAR + v, column),
+            get_field,
             lambda column: load(SX, column),
             lambda column: load(SY, column),
             put,
@@ -162,11 +170,8 @@
         )
 
     for h in range(2):
-        for unit in range(4):
-            for i in range(2):
-                halo_copy(h, i, unit).wait_recv()
-            if unit >= VAR:
-                run_block(h, unit - VAR)
+        for v in range(2):
+            run_block(h, v)
 
     def slot(b):
         return win_ref.at[pl.ds(pl.multiple_of(b * 64, 64), 64)]
@@ -187,17 +192,18 @@
     def send(i, carry):
         b = target(i)
         start = st[b]
+        place = (lane + (256 - start)) & 127
+        top, second, fourth = place < 64, place < 32, place < 96
+        low = ((lane + 128 - 32 * (place // 32)) & 127) >= start
         for c in range(WIDTH):
-            parts = []
-            for q in range(4):
-                v, h = q // 2, q % 2
-                x = jnp.where(lane >= start, done[h, c, v, 0], done[h, c, v, 1])
-                parts.append(roll(x, (32 * q + 256 - start) & 127))
-            send_buf[i, pl.ds(c * 8, 8), :] = jnp.where(
-                lane < 64,
-                jnp.where(lane < 32, parts[0], parts[1]),
-                jnp.where(lane < 96, parts[2], parts[3]),
-            )
+            both = []
+            for half in range(2):
+                x = [done[c, q, half] for q in range(4)]
+                both.append(
+                    jnp.where(top, jnp.where(second, x[0], x[1]), jnp.where(fourth, x[2], x[3]))
+                )
+            x = jnp.where(low, both[0], both[1])
+            send_buf[i, pl.ds(c * 8, 8), :] = roll(x, (256 - start) & 127)
 
         @pl.when(b != band)
         def _():
@@ -286,7 +292,6 @@
 
 def shards(background, scale_x, scale_y, filter_bands, band_rows):
     f32 = jnp.float32
-    any_space = pl.BlockSpec(memory_space=pl.ANY)
     hbm = pl.BlockSpec(memory_space=pltpu.HBM)
     resident = pl.BlockSpec(memory_space=pltpu.VMEM)
     vmem = pltpu.VMEM
@@ -307,7 +312,7 @@
         scratch_shapes=[
             vmem((4, 2, 128, LANES), f32),
             vmem((3, 2, 4, WIDTH, 2, 8, LANES), f32),
-            vmem((2, WIDTH, 2, 2, 8, LANES), f32),
+            vmem((WIDTH, 4, 2, 8, LANES), f32),
             vmem((512, LANES), f32),
             vmem((16, 64, LANES), f32),
             pltpu.SMEM((16,), jnp.int32),
@@ -336,7 +341,7 @@
             jax.ShapeDtypeStruct((512, LANES), f32),
             jax.ShapeDtypeStruct((1024, LANES), f32),
         ),
-        in_specs=[any_space, any_space, resident, resident],
+        in_specs=[hbm, hbm, resident, resident],
         out_specs=(hbm, hbm),
         scratch_shapes=[
             pltpu.SMEM((16,), jnp.int32),
@@ -347,7 +352,7 @@
             dma((3,)),
         ],
         compiler_params=pltpu.CompilerParams(vmem_limit_bytes=16 << 20),
-    )(band_rows, filters, win, inc)
+    )(stay(band_rows), stay(filters), win, inc)
     inc = jnp.transpose(inc.reshape(32, 2, 8, LANES), (0, 2, 1, 3))
     return inc.reshape(background.shape), bf.reshape(2, 16, CAP, LANES)
 

time: 31.6 us -> 31 us (0.981)
  local copies, waits for them, and re-layouts: 0.64 us -> 0 us
    unnamed x4 -> x0, local copies, waits for them, and re-layouts: 0.64 us -> none
where the time goes in v4:
time: 31 us; the launch traced here: 30.9 us
  Pallas kernels  30.2 us (97%)
  between operations  0.64 us (2%)
    pallas_call x1, Pallas kernels, shards(): pl.pallas_call(strips_kernel, out_shape=(jax.ShapeDtypeStruct((1024, LANE...  28.5 us
    pallas_call x1, Pallas kernels, shards(): pl.pallas_call(filter_kernel, out_shape=(jax.ShapeDtypeStruct((512, LANES...  1.72 us

profile of v4, /device:TPU:0, one launch (start us, length us, event | category | flops | bytes accessed | tf_op | source)
XLA Modules:
  0.0 30.9 jit_solution(17753193374341328212)
XLA Ops:
  0.6 28.5 %shard_map.68 = (f32[1024,128]{1,0:T(8,128)S(1)}, f32[512,128]{1,0:T(8,128)S(1)}) custom-call(s32[16]{0:T(128)} %rows_ref.3, f32[5,2,16]{2,1,0:T(2,128)} %bitcast.25, f32[2,2,128,128]{3,2,1,0:T(8,128)} %bitcast.22, f32[2,128,128]{2,1,0:T(8,128)} %bitcast.23, f32[2,128,128]{2,1,0:T(8,128)} %bitcast.24), custom_call_target="tpu_custom_call" | custom-call | tf_op jit(solution)/shard_map/pallas_call | solution.py:304
  29.1 1.7 %shard_map.69 = (f32[512,128]{1,0:T(8,128)}, f32[1024,128]{1,0:T(8,128)}) custom-call(s32[16]{0:T(128)} %rows_ref.3, f32[5,2,16]{2,1,0:T(2,128)} %bitcast.26, f32[1024,128]{1,0:T(8,128)S(1)} %get-tuple-element.6.win_ref, f32[512,128]{1,0:T(8,128)S(1)} %get-tuple-element.7.inc_ref), custom_call_target="tpu_custom_call" | custom-call | tf_op jit(solution)/shard_map/pallas_call | solution.py:338

commit v5 on v4

--- a/solution.py
+++ b/solution.py
@@ -18,7 +18,7 @@
     return pltpu.roll(x, shift, x.ndim - 1)
 
 
-def diffuse(get_field, get_sx, get_sy, put, lane):
+def diffuse(get_field, get_sx, get_sy, get_behind, put, lane):
     last, first = lane == LANES - 1, lane == 0
     held = [None] * STEPS
     flux = [None] * STEPS
@@ -37,12 +37,13 @@
         flux[step] = east
         if west is None:
             return
-        sy = get_sy(p)
+        sy, behind = get_sy(p), get_behind(p)
         ra, rb = roll(before[0], LANES - 1), roll(before[1], LANES - 1)
         up = [jnp.where(last, rb, ra), rb]
+        qa, qb = roll(before[0], 1), roll(before[1], 1)
+        down = [qa, jnp.where(first, qa, qb)]
         north = [sy[i] * (up[i] - before[i]) for i in range(2)]
-        qa, qb = roll(north[0], 1), roll(north[1], 1)
-        south = [jnp.where(first, qb, qa), jnp.where(first, qa, qb)]
+        south = [behind[i] * (before[i] - down[i]) for i in range(2)]
         new = [before[i] + east[i] - west[i] + north[i] - south[i] for i in range(2)]
         push(step + 1, p, new)
 
@@ -63,7 +64,7 @@
 def strips_kernel(
     rows_ref, filt_ref, bg_ref, sx_ref, sy_ref,
     win_ref, inc_ref,
-    raw, cols, done, nat, send_buf, rows, filt, st,
+    raw, cols, row_behind, done, nat, send_buf, rows, filt, st,
     near_sem, in_sem, hs_sem, hr_sem, as_sem, ar_sem,
 ):
     n_band, n_lon = lax.axis_size("band"), lax.axis_size("lon")
@@ -154,17 +155,23 @@
                 row = ((v * 16 + h * 8) * 2 + half) * 8 + column
                 nat[pl.ds(row, 8, stride=16), :] = new[half]
 
-        def get_field(column):
-            if column == -WIDTH:
-                for i in range(2):
-                    for unit in ((SX, SY, VAR), (VAR + 1,))[v]:
-                        halo_copy(h, i, unit).wait_recv()
-            return load(VAR + v, column)
+        if v == 0:
+            for i in range(2):
+                halo_copy(h, i, SX).wait_recv()
+                halo_copy(h, i, SY).wait_recv()
+            for column in range(1 - WIDTH, 2 * WIDTH - 1):
+                low, high = load(SY, column)
+                low, high = roll(low, 1), roll(high, 1)
+                row_behind[h, column + WIDTH, 0] = jnp.where(lane == 0, high, low)
+                row_behind[h, column + WIDTH, 1] = jnp.where(lane == 0, low, high)
+        for i in range(2):
+            halo_copy(h, i, VAR + v).wait_recv()
 
         diffuse(
-            get_field,
+            lambda column: load(VAR + v, column),
             lambda column: load(SX, column),
             lambda column: load(SY, column),
+            lambda column: [row_behind[h, column + WIDTH, half] for half in range(2)],
             put,
             lane,
         )
@@ -177,7 +184,7 @@
         return win_ref.at[pl.ds(pl.multiple_of(b * 64, 64), 64)]
 
     def target(i):
-        return i // 4 * 4 + lax.rem(lax.rem(band, 4) + lax.rem(i, 4), 4)
+        return i
 
     def band_copy(i):
         return pltpu.make_async_remote_copy(
@@ -312,6 +319,7 @@
         scratch_shapes=[
             vmem((4, 2, 128, LANES), f32),
             vmem((3, 2, 4, WIDTH, 2, 8, LANES), f32),
+            vmem((2, 3 * WIDTH, 2, 8, LANES), f32),
             vmem((WIDTH, 4, 2, 8, LANES), f32),
             vmem((512, LANES), f32),
             vmem((16, 64, LANES), f32),

time: 31 us -> 30.3 us (0.977)
  Pallas kernels: 30.2 us -> 29.4 us
    pallas_call x1, Pallas kernels: 28.5 us -> 27.7 us  [shards(): pl.pallas_call(strips_kernel, out_shape=(jax.ShapeDtypeStruct((1024, LANE...]
where the time goes in v5:
time: 30.3 us; the launch traced here: 30.1 us
  Pallas kernels  29.4 us (97%)
  between operations  0.64 us (2%)
    pallas_call x1, Pallas kernels, shards(): pl.pallas_call(strips_kernel, out_shape=(jax.ShapeDtypeStruct((1024, LANE...  27.7 us
    pallas_call x1, Pallas kernels, shards(): pl.pallas_call(filter_kernel, out_shape=(jax.ShapeDtypeStruct((512, LANES...  1.72 us

profile of v5, /device:TPU:0, one launch (start us, length us, event | category | flops | bytes accessed | tf_op | source)
XLA Modules:
  0.0 30.1 jit_solution(74949626372491858)
XLA Ops:
  0.6 27.7 %shard_map.68 = (f32[1024,128]{1,0:T(8,128)S(1)}, f32[512,128]{1,0:T(8,128)S(1)}) custom-call(s32[16]{0:T(128)} %rows_ref.3, f32[5,2,16]{2,1,0:T(2,128)} %bitcast.25, f32[2,2,128,128]{3,2,1,0:T(8,128)} %bitcast.22, f32[2,128,128]{2,1,0:T(8,128)} %bitcast.23, f32[2,128,128]{2,1,0:T(8,128)} %bitcast.24), custom_call_target="tpu_custom_call" | custom-call | tf_op jit(solution)/shard_map/pallas_call | solution.py:311
  28.3 1.7 %shard_map.69 = (f32[512,128]{1,0:T(8,128)}, f32[1024,128]{1,0:T(8,128)}) custom-call(s32[16]{0:T(128)} %rows_ref.3, f32[5,2,16]{2,1,0:T(2,128)} %bitcast.26, f32[1024,128]{1,0:T(8,128)S(1)} %get-tuple-element.6.win_ref, f32[512,128]{1,0:T(8,128)S(1)} %get-tuple-element.7.inc_ref), custom_call_target="tpu_custom_call" | custom-call | tf_op jit(solution)/shard_map/pallas_call | solution.py:346

commit v6 on v5

--- a/solution.py
+++ b/solution.py
@@ -222,7 +222,7 @@
 
         return carry
 
-    lax.fori_loop(0, n_band, send, 0)
+    lax.fori_loop(0, n_band, send, 0, unroll=2)
 
     for v in range(2):
         for level in range(16):
@@ -258,7 +258,7 @@
     rows_ref, filt_ref, win_ref, inc_ref, out_inc_ref, bf_ref,
     rows, filt, band_nat, out_bf, in_sem, out_sem,
 ):
-    outs = [pltpu.make_async_copy(inc_ref, out_inc_ref, out_sem.at[2])]
+    outs = [pltpu.make_async_copy(inc_ref, out_inc_ref, out_sem.at[4])]
     scalars = [
         pltpu.make_async_copy(rows_ref, rows, in_sem.at[0]),
         pltpu.make_async_copy(filt_ref, filt, in_sem.at[1]),
@@ -282,12 +282,14 @@
                     value = value + filt[o, v, level] * band_nat[v, level + o - 2]
             at = (v * 16 + level) * CAP
             out_bf[at:at + CAP, :] = jnp.where(inside, value, 0.0)
-        outs.append(
-            pltpu.make_async_copy(
-                out_bf.at[pl.ds(v * 512, 512)], bf_ref.at[pl.ds(v * 512, 512)], out_sem.at[v]
-            )
-        )
-        outs[-1].start()
+            if level % 8 == 7:
+                part = pl.ds(at - 7 * CAP, 8 * CAP)
+                outs.append(
+                    pltpu.make_async_copy(
+                        out_bf.at[part], bf_ref.at[part], out_sem.at[2 * v + level // 8]
+                    )
+                )
+                outs[-1].start()
     for copy in outs:
         copy.wait()
 
@@ -357,7 +359,7 @@
             vmem((2, 16, CAP, LANES), f32),
             vmem((1024, LANES), f32),
             dma((2,)),
-            dma((3,)),
+            dma((5,)),
         ],
         compiler_params=pltpu.CompilerParams(vmem_limit_bytes=16 << 20),
     )(stay(band_rows), stay(filters), win, inc)

time: 30.3 us -> 30.3 us (level)
  no operation moved by 1% of the time
where the time goes in v6:
time: 30.3 us; the launch traced here: 30 us
  Pallas kernels  29.4 us (97%)
  between operations  0.64 us (2%)
    pallas_call x1, Pallas kernels, shards(): pl.pallas_call(strips_kernel, out_shape=(jax.ShapeDtypeStruct((1024, LANE...  27.7 us
    pallas_call x1, Pallas kernels, shards(): pl.pallas_call(filter_kernel, out_shape=(jax.ShapeDtypeStruct((512, LANES...  1.69 us

profile of v6, /device:TPU:0, one launch (start us, length us, event | category | flops | bytes accessed | tf_op | source)
XLA Modules:
  0.0 30.0 jit_solution(13170201653199963909)
XLA Ops:
  0.6 27.7 %shard_map.68 = (f32[1024,128]{1,0:T(8,128)S(1)}, f32[512,128]{1,0:T(8,128)S(1)}) custom-call(s32[16]{0:T(128)} %rows_ref.3, f32[5,2,16]{2,1,0:T(2,128)} %bitcast.25, f32[2,2,128,128]{3,2,1,0:T(8,128)} %bitcast.22, f32[2,128,128]{2,1,0:T(8,128)} %bitcast.23, f32[2,128,128]{2,1,0:T(8,128)} %bitcast.24), custom_call_target="tpu_custom_call" | custom-call | tf_op jit(solution)/shard_map/pallas_call | solution.py:313
  28.3 1.7 %shard_map.69 = (f32[512,128]{1,0:T(8,128)}, f32[1024,128]{1,0:T(8,128)}) custom-call(s32[16]{0:T(128)} %rows_ref.3, f32[5,2,16]{2,1,0:T(2,128)} %bitcast.26, f32[1024,128]{1,0:T(8,128)S(1)} %get-tuple-element.6.win_ref, f32[512,128]{1,0:T(8,128)S(1)} %get-tuple-element.7.inc_ref), custom_call_target="tpu_custom_call" | custom-call | tf_op jit(solution)/shard_map/pallas_call | solution.py:348
